TPU v7x, 512 devices: a whole 4x8x8 slice. The times are simulated.
512 devices in a mesh: grid: 16 (over y, core), dom: 32 (over z, x).
Axes of the slice: x: 4, y: 8, z: 8, core: 2. Of those that a mesh axis runs over, the one named last changes fastest.
Arguments:
- state: float32 [5, 125, 65536], P(None, None, ('grid', 'dom')), as said below
- inv_size: float32 [3, 65536], P(None, ('grid', 'dom')), may hold values from 1 to 4
- plus_order: int32 [3, 65536], P(None, ('grid', 'dom')), may hold values from 0 to 127, as said below
- minus_order: int32 [3, 65536], P(None, ('grid', 'dom')), may hold values from 0 to 127, as said below
- donor_cell: int32 [512, 1024], P(('grid', 'dom')), may hold values from 0 to 127
- donor_weights: float32 [512, 3, 5, 1024], P(('grid', 'dom')), as said below
- recv_slot: int32 [512, 600], P(('grid', 'dom')), may hold values from 0 to 1023, as said below
Outputs:
- rhs: float32 [5, 125, 65536], P(None, None, ('grid', 'dom'))
Inputs may be any that keep to these rules, and one draw needn't show every extreme that they name: `plus_order`: within each device's block of 128 columns, every row is a permutation of the local element numbers. `minus_order`: within each device's block of 128 columns, every row is a permutation of the local element numbers. `state`: density lies in [0.9, 1.1], each momentum in [-0.1, 0.1], energy in [2.4, 2.6]. `donor_weights`: for each donor device, direction and slot, the five weights are the Lagrange basis of the five Gauss-Legendre points evaluated at one coordinate in [-0.8, 0.8]. `recv_slot`: entries of one device's row are distinct, and each names a slot whose source device (the slot // 2) lies in another grid than the row's device.
All inputs are finite; a program needn't handle non-finite values.
Results may differ from a plain program's by a relative error of at most 0.0003.
Values sent between devices are 32-bit elements; how exact they have to be, the bound alone decides.
A program may use at most 64 MiB of HBM per device.

v0:
```python
import math

import jax
import jax.numpy as jnp
from jax import lax
from jax.sharding import PartitionSpec as P

precise = lax.Precision.HIGHEST
volume_forms = ("ia,vabce->vibce", "ib,vabce->vaice", "ic,vabce->vabie")
face_forms = ("a,vabce->vbce", "b,vabce->vace", "c,vabce->vabe")
lift_forms = ("i,vbce->vibce", "i,vace->vaice", "i,vabe->vabie")


def gauss_nodes():
    outer = math.sqrt(5.0 + 2.0 * math.sqrt(10.0 / 7.0)) / 3.0
    inner = math.sqrt(5.0 - 2.0 * math.sqrt(10.0 / 7.0)) / 3.0
    return [-outer, -inner, 0.0, inner, outer]


def basis_value(nodes, column, target_positions):
    value = 1.0
    for other in range(5):
        if other != column:
            value = value * (target_positions - nodes[other]) / (nodes[column] - nodes[other])
    return value


def basis_slope(nodes, column, target_positions):
    total = 0.0
    for skipped in range(5):
        if skipped != column:
            value = 1.0 / (nodes[column] - nodes[skipped])
            for other in range(5):
                if other != column and other != skipped:
                    value = (
                        value * (target_positions - nodes[other]) / (nodes[column] - nodes[other])
                    )
            total = total + value
    return total


def legendre_slopes(target_positions):
    values = [1.0, target_positions]
    slopes = [0.0, 1.0]
    for order in range(1, 5):
        values.append(
            ((2 * order + 1) * target_positions * values[order] - order * values[order - 1])
            / (order + 1)
        )
        slopes.append(slopes[order - 1] + (2 * order + 1) * values[order])
    return (slopes[4], slopes[5])


def tables():
    nodes = gauss_nodes()
    deriv = [[basis_slope(nodes, column, nodes[row]) for column in range(5)] for row in range(5)]
    lower = [basis_value(nodes, column, -1.0) for column in range(5)]
    upper = [basis_value(nodes, column, 1.0) for column in range(5)]
    lift_low = []
    lift_high = []
    for row in range(5):
        slope_four, slope_five = legendre_slopes(nodes[row])
        lift_low.append(-0.5 * (slope_five - slope_four))
        lift_high.append(0.5 * (slope_five + slope_four))
    return tuple(
        (jnp.asarray(matrix, jnp.float32) for matrix in (deriv, lower, upper, lift_low, lift_high))
    )


def euler_flux(state, direction):
    density = state[0]
    momenta = state[1:4]
    energy = state[4]
    speed = momenta[direction] / density
    pressure = 0.4 * (energy - 0.5 * jnp.sum(momenta * momenta, axis=0) / density)
    pieces = [
        momenta[direction],
        momenta[0] * speed,
        momenta[1] * speed,
        momenta[2] * speed,
        (energy + pressure) * speed,
    ]
    pieces[1 + direction] = pieces[1 + direction] + pressure
    sound = jnp.sqrt(1.4 * pressure / density)
    return (jnp.stack(pieces), jnp.abs(speed) + sound)


def common_flux(left_state, right_state, direction):
    left_flux, left_wave = euler_flux(left_state, direction)
    right_flux, right_wave = euler_flux(right_state, direction)
    wave = jnp.maximum(left_wave, right_wave)
    return 0.5 * (left_flux + right_flux) - 0.5 * wave * (right_state - left_state)


def remote_fluxes(left_states, right_states):
    return jnp.stack(
        [
            common_flux(left_states[direction], right_states[direction], direction)
            for direction in range(3)
        ]
    )


def slot_states(state, plus_rows, minus_rows):
    deriv, lower, upper, lift_low, lift_high = tables()
    columns = state.shape[-1]
    grid_form = state.reshape(5, 5, 5, 5, columns)
    high_slots = []
    low_slots = []
    for direction in range(3):
        high_face = jnp.einsum(face_forms[direction], upper, grid_form, precision=precise).reshape(
            5, 25, columns
        )
        low_face = jnp.einsum(face_forms[direction], lower, grid_form, precision=precise).reshape(
            5, 25, columns
        )
        high_slots.append(jnp.take(high_face, plus_rows[direction], axis=2))
        low_slots.append(jnp.take(low_face, minus_rows[direction], axis=2))
    return (jnp.stack(high_slots), jnp.stack(low_slots))


def interpolate(state, cells, weights, blocks):
    block_width = cells.shape[0] // blocks

    def one_block(index):
        block_cells = lax.dynamic_slice_in_dim(cells, index * block_width, block_width)
        block_weights = lax.dynamic_slice_in_dim(weights, index * block_width, block_width, axis=2)
        gathered = jnp.take(state, block_cells, axis=2).reshape(5, 5, 5, 5, block_width)
        reduced = jnp.einsum("as,vabcs->vbcs", block_weights[0], gathered, precision=precise)
        reduced = jnp.einsum("bs,vbcs->vcs", block_weights[1], reduced, precision=precise)
        return jnp.einsum("cs,vcs->vs", block_weights[2], reduced, precision=precise)

    values = lax.map(one_block, jnp.arange(blocks, dtype=jnp.int32))
    return jnp.transpose(values, (1, 0, 2)).reshape(5, blocks * block_width)


def inverse_order(rows):
    count = rows.shape[0]
    return jnp.zeros((count,), jnp.int32).at[rows].set(jnp.arange(count, dtype=jnp.int32))


def assemble(high_slots, low_slots, remote_plus, remote_minus, fringe, plus_rows, minus_rows):
    remote = remote_plus.shape[-1]
    start = remote + fringe.shape[-1]
    plus_parts = []
    minus_parts = []
    for direction in range(3):
        local_flux = common_flux(
            high_slots[direction][:, :, start:], low_slots[direction][:, :, start:], direction
        )
        fringe_high = common_flux(
            high_slots[direction][:, :, remote:start], fringe[direction, 1], direction
        )
        fringe_low = common_flux(
            fringe[direction, 0], low_slots[direction][:, :, remote:start], direction
        )
        plus_slots = jnp.concatenate([remote_plus[direction], fringe_high, local_flux], axis=2)
        minus_slots = jnp.concatenate([remote_minus[direction], fringe_low, local_flux], axis=2)
        plus_parts.append(jnp.take(plus_slots, inverse_order(plus_rows[direction]), axis=2))
        minus_parts.append(jnp.take(minus_slots, inverse_order(minus_rows[direction]), axis=2))
    return (jnp.stack(plus_parts), jnp.stack(minus_parts))


def divergence(state, scales, plus_common, minus_common):
    deriv, lower, upper, lift_low, lift_high = tables()
    columns = state.shape[-1]
    grid_form = state.reshape(5, 5, 5, 5, columns)
    total = jnp.zeros_like(grid_form)
    for direction in range(3):
        flux = euler_flux(grid_form, direction)[0]
        inner = jnp.einsum(volume_forms[direction], deriv, flux, precision=precise)
        low_jump = minus_common[direction].reshape(5, 5, 5, columns) - jnp.einsum(
            face_forms[direction], lower, flux, precision=precise
        )
        high_jump = plus_common[direction].reshape(5, 5, 5, columns) - jnp.einsum(
            face_forms[direction], upper, flux, precision=precise
        )
        inner = inner + jnp.einsum(lift_forms[direction], lift_low, low_jump, precision=precise)
        inner = inner + jnp.einsum(lift_forms[direction], lift_high, high_jump, precision=precise)
        total = total + scales[direction] * inner
    return (-total).reshape(5, 125, columns)


def body(state, inv_size, plus_order, minus_order, donor_cell, donor_weights, recv_slot):
    columns = state.shape[-1]
    part_count = lax.axis_size("dom")
    grid_count = lax.axis_size("grid")
    capacity = max(1, columns // (3 * part_count))
    remote = part_count * capacity
    fringe_count = recv_slot.shape[-1] // 150
    high_slots, low_slots = slot_states(state, plus_order, minus_order)
    values = interpolate(state, donor_cell[0], donor_weights[0], grid_count)
    slot_count = values.shape[1] // (grid_count * part_count)
    shaped = values.reshape(5, grid_count, part_count, slot_count)
    arrived = lax.all_to_all(
        lax.all_to_all(shaped, "grid", split_axis=1, concat_axis=1, tiled=True),
        "dom",
        split_axis=2,
        concat_axis=2,
        tiled=True,
    )
    arrived = arrived.reshape(5, grid_count * part_count * slot_count)
    fringe = jnp.take(arrived, recv_slot[0], axis=1)
    fringe = jnp.transpose(fringe.reshape(5, 3, 2, 25, fringe_count), (1, 2, 0, 3, 4))
    own_high = high_slots[..., :remote]
    own_low = low_slots[..., :remote]
    outgoing = own_low.reshape(3, 5, 25, part_count, capacity)
    partner_low = lax.all_to_all(outgoing, "dom", split_axis=3, concat_axis=3, tiled=True).reshape(
        3, 5, 25, remote
    )
    remote_plus = remote_fluxes(own_high, partner_low)
    returned = lax.all_to_all(
        remote_plus.reshape(3, 5, 25, part_count, capacity),
        "dom",
        split_axis=3,
        concat_axis=3,
        tiled=True,
    )
    remote_minus = returned.reshape(3, 5, 25, remote)
    plus_common, minus_common = assemble(
        high_slots, low_slots, remote_plus, remote_minus, fringe, plus_order, minus_order
    )
    return divergence(state, inv_size, plus_common, minus_common)


def solution(mesh):
    return jax.shard_map(
        body,
        mesh=mesh,
        in_specs=(
            P(None, None, ("grid", "dom")),
            P(None, ("grid", "dom")),
            P(None, ("grid", "dom")),
            P(None, ("grid", "dom")),
            P(("grid", "dom"), None),
            P(("grid", "dom"), None, None, None),
            P(("grid", "dom"), None),
        ),
        out_specs=P(None, None, ("grid", "dom")),
        check_vma=False,
    )
```

profile of v0, /device:TPU:1, one launch (start us, length us, event | category | flops | bytes accessed | tf_op | source)
XLA Modules:
  0.0 253.6 jit_solution(12432255003614025478)
XLA Ops:
  1.3 58.2 %while.10 = (s32[]{:T(128)}, f32[16,5,64]{2,1,0:T(8,128)S(1)}, s32[16]{0:T(128)S(1)}, s32[1024]{0:T(1024)}, f32[5,125,128]{1,0,2:T(8,128)S(1)}, /*index=5*/f32[3...) while((s32[]{:T(128)}, f32[16,5,64]{2,1,0:T(8,128)S(1)}, ...), condition=%wide.region_8.10_spmd, body=%wide.region_7.9_spmd.sunk | while | flops 130696 | bytes 1246307 | solution.py:133
  60.5 10.7 %all-to-all-start.2 = ((f32[16,1,320]{2,1,0:T(1,128)}), f32[16,1,320]{2,1,0:T(1,128)}, u32[]{:S(2)}, u32[]{:S(2)}) async-start(f32[16,1,320]{2,1,0:T(1,128)} %reshape.3685), calls=%async_computation.2 | async-start | bytes 49152 | tf_op jit(solution)/shard_map/all_to_all | solution.py:196
  114.1 1.2 fusion.20
  115.3 1.2 fusion.18
  119.4 2.5 gather_fusion.5
  122.5 1.9 fusion.39
  127.7 1.2 scatter_custom_fusion.5
  130.1 1.4 fusion.22
  131.5 1.4 fusion.16
  132.9 1.2 fusion.12
  136.3 1.2 fusion.14
  162.0 1.7 fusion.30
  165.5 1.4 reduce.22
  168.1 11.3 %all-to-all-start.3 = ((f32[32,1,160]{2,1,0:T(1,128)}), f32[32,1,160]{2,1,0:T(1,128)}, u32[]{:S(2)}, u32[]{:S(2)}) async-start(f32[32,1,160]{2,1,0:T(1,128)} %reshape.3687), calls=%async_computation.3 | async-start | bytes 65536 | tf_op jit(solution)/shard_map/all_to_all | solution.py:195
  181.1 1.3 reduce.24
  184.2 3.7 %all-to-all-done.3 = f32[32,1,160]{2,1,0:T(1,128)} async-done(((f32[32,1,160]{2,1,0:T(1,128)}), f32[32,1,160]{2,1,0:T(1,128)}, u32[]{:S(2)}, u32[]{:S(2)}) %all-to-all-start.3) | async-done | bytes 20512 | tf_op jit(solution)/shard_map/all_to_all | solution.py:195
  188.0 5.3 %all-to-all-start = ((f32[32,1,375]{2,1,0:T(1,128)}), f32[32,1,375]{2,1,0:T(1,128)}, u32[]{:S(2)}, u32[]{:S(2)}) async-start(f32[32,1,375]{2,1,0:T(1,128)} %reshape.3689), calls=%async_computation | async-start | bytes 98304 | tf_op jit(solution)/shard_map/all_to_all | solution.py:208
  193.3 1.5 reduce.23
  195.6 1.8 copy.2745
  197.4 2.3 gather_fusion.1
  204.3 1.5 reduce.25
  210.9 1.3 reduce.26
  212.9 9.4 %all-to-all-start.1 = ((f32[32,1,375]{2,1,0:T(1,128)}), f32[32,1,375]{2,1,0:T(1,128)S(1)}, u32[]{:S(2)}, u32[]{:S(2)}) async-start(f32[32,1,375]{2,1,0:T(1,128)} %reshape.3691), calls=%async_computation.1 | async-start | bytes 98304 | tf_op jit(solution)/shard_map/all_to_all | solution.py:212
  225.8 5.1 %all-to-all-done.1 = f32[32,1,375]{2,1,0:T(1,128)S(1)} async-done(((f32[32,1,375]{2,1,0:T(1,128)}), f32[32,1,375]{2,1,0:T(1,128)S(1)}, u32[]{:S(2)}, u32[]{:S(2)}) %all-to-all-start.1) | async-done | bytes 48032 | tf_op jit(solution)/shard_map/all_to_all | solution.py:212
  (865 shorter events, 168.9 us)
Async XLA Ops:
  59.5 11.7 %copy-start = (f32[5,125,128]{2,1,0:T(8,128)S(1)}, f32[5,125,128]{2,1,0:T(8,128)}, u32[]{:S(2)}) copy-start(f32[5,125,128]{2,1,0:T(8,128)} %param.18) | copy-start | bytes 960004
  60.5 104.5 %all-to-all-start.2 = ((f32[16,1,320]{2,1,0:T(1,128)}), f32[16,1,320]{2,1,0:T(1,128)}, u32[]{:S(2)}, u32[]{:S(2)}) async-start(f32[16,1,320]{2,1,0:T(1,128)} %reshape.3685), calls=%async_computation.2 | async-start | bytes 49152 | tf_op jit(solution)/shard_map/all_to_all | solution.py:196
  94.0 4.6 %copy-start.41 = (f32[1,5,25,128]{3,0,2,1:T(1,128)S(1)}, f32[1,5,25,128]{3,0,2,1:T(1,128)}, u32[]{:S(2)}) copy-start(f32[1,5,25,128]{3,0,2,1:T(1,128)} %fusion.220) | copy-start | bytes 192004
  127.7 2.4 copy-start.93
  139.5 1.9 copy-start.72
  139.6 2.5 %copy-start.7 = (f32[1,5,25,128]{2,3,1,0:T(8,128)S(1)}, f32[1,5,25,128]{2,3,1,0:T(8,128)}, u32[]{:S(2)}) copy-start(f32[1,5,25,128]{2,3,1,0:T(8,128)} %get-tuple-element.210) | copy-start | bytes 192004
  141.3 17.4 %copy-start.17 = (f32[1,1,25,32]{2,3,1,0:T(8,128)}, f32[1,1,25,32]{2,3,1,0:T(8,128)S(1)}, u32[]{:S(2)}) copy-start(f32[1,1,25,32]{2,3,1,0:T(8,128)S(1)} %copy.2908) | copy-start | bytes 9604
  141.4 17.3 %copy-start.19 = (f32[25,32]{0,1:T(8,128)}, f32[25,32]{0,1:T(8,128)S(1)}, u32[]{:S(2)}) copy-start(f32[25,32]{0,1:T(8,128)S(1)} %copy.2728) | copy-start | bytes 9604
  144.5 1.7 copy-start.69
  145.4 10.4 %copy-start.21 = (f32[1,1,25,32]{2,3,1,0:T(8,128)}, f32[1,1,25,32]{2,3,1,0:T(8,128)S(1)}, u32[]{:S(2)}) copy-start(f32[1,1,25,32]{2,3,1,0:T(8,128)S(1)} %copy.2895) | copy-start | bytes 9604
  145.5 10.3 %copy-start.23 = (f32[25,32]{0,1:T(8,128)}, f32[25,32]{0,1:T(8,128)S(1)}, u32[]{:S(2)}) copy-start(f32[25,32]{0,1:T(8,128)S(1)} %copy.2712) | copy-start | bytes 9604
  147.0 2.6 %copy-start.25 = (f32[1,1,25,32]{2,3,1,0:T(8,128)}, f32[1,1,25,32]{2,3,1,0:T(8,128)S(1)}, u32[]{:S(2)}) copy-start(f32[1,1,25,32]{2,3,1,0:T(8,128)S(1)} %copy.2882) | copy-start | bytes 9604
  147.2 2.4 copy-start.27
  152.9 2.0 copy-start.31
  153.6 2.3 copy-start.115
  155.7 1.8 copy-start.2
  157.8 2.3 copy-start.30
  167.3 12.2 %copy-start.126 = (s32[128]{0:T(128)S(1)}, s32[128]{0:T(128)}, u32[]{:S(2)}) copy-start(s32[128]{0:T(128)} %compare_select_fusion.3) | copy-start | bytes 1540
  167.3 12.2 %copy-start.127 = (s32[128]{0:T(128)S(1)}, s32[128]{0:T(128)}, u32[]{:S(2)}) copy-start(s32[128]{0:T(128)} %compare_select_fusion.4) | copy-start | bytes 1540
  167.3 12.8 %copy-start.75 = (pred[3,2,25,4]{3,2,1,0:T(8,128)(4,1)S(1)}, pred[3,2,25,4]{3,2,1,0:T(8,128)(4,1)}, u32[]{:S(2)}) copy-start(pred[3,2,25,4]{3,2,1,0:T(8,128)(4,1)} %compare_and_fusion.1) | copy-start | bytes 1804
  168.1 12.1 %copy-start.9 = (f32[5,25,128]{2,1,0:T(8,128)S(1)}, f32[5,25,128]{2,1,0:T(8,128)}, u32[]{:S(2)}) copy-start(f32[5,25,128]{2,1,0:T(8,128)} %copy-done.8) | copy-start | bytes 192004
  168.1 19.9 %all-to-all-start.3 = ((f32[32,1,160]{2,1,0:T(1,128)}), f32[32,1,160]{2,1,0:T(1,128)}, u32[]{:S(2)}, u32[]{:S(2)}) async-start(f32[32,1,160]{2,1,0:T(1,128)} %reshape.3687), calls=%async_computation.3 | async-start | bytes 65536 | tf_op jit(solution)/shard_map/all_to_all | solution.py:195
  188.0 16.3 %all-to-all-start = ((f32[32,1,375]{2,1,0:T(1,128)}), f32[32,1,375]{2,1,0:T(1,128)}, u32[]{:S(2)}, u32[]{:S(2)}) async-start(f32[32,1,375]{2,1,0:T(1,128)} %reshape.3689), calls=%async_computation | async-start | bytes 98304 | tf_op jit(solution)/shard_map/all_to_all | solution.py:208
  212.9 17.9 %all-to-all-start.1 = ((f32[32,1,375]{2,1,0:T(1,128)}), f32[32,1,375]{2,1,0:T(1,128)S(1)}, u32[]{:S(2)}, u32[]{:S(2)}) async-start(f32[32,1,375]{2,1,0:T(1,128)} %reshape.3691), calls=%async_computation.1 | async-start | bytes 98304 | tf_op jit(solution)/shard_map/all_to_all | solution.py:212
  (108 other events, 92.5 us)
where the time goes:
time: 258 us; the launch traced here: 254 us
  local copies, waits for them, and re-layouts  120 us (47%)
  other arithmetic  60 us (23%)
  starting transfers between devices  36.7 us (14%)
  matrix products  15.5 us (6%)
  loops' own time  10.8 us (4%)
  waiting for transfers between devices  8.82 us (3%)
    unnamed x296, local copies, waits for them, and re-layouts  47.7 us
    gather x48, local copies, waits for them, and re-layouts, one_block(): jnp.take(state, block_cells, axis=2).reshape(5, 5, 5, 5, block_width)  14.1 us
    and x16, other arithmetic, one_block(): jnp.take(state, block_cells, axis=2).reshape(5, 5, 5, 5, block_width)  12.3 us
    all_to_all x1, starting transfers between devices, body(): lax.all_to_all(lax.all_to_all(shaped, 'grid', split_axis=1, concat_axis=1...  11.3 us
    another operation x1, loops' own time, interpolate(): values = lax.map(one_block, jnp.arange(blocks, dtype=jnp.int32))  10.8 us
    all_to_all x1, starting transfers between devices, body(): lax.all_to_all(shaped, 'grid', split_axis=1, concat_axis=1, tiled=True)  10.7 us
    reduce_sum x18, other arithmetic, euler_flux(): jnp.sum(momenta * momenta, axis=0)  10.1 us
    dynamic_slice x16, local copies, waits for them, and re-layouts, interpolate(): values = lax.map(one_block, jnp.arange(blocks, dtype=jnp.int32))  9.94 us
  transfers between devices with their start and end apart: 4, of which 2 were waited for; matrix products, arithmetic and copies ran while one was open for 34% of the time, Pallas kernels for 0%

commit v1 on v0

v1 whole, which is shorter than its diff:
```python
import functools
import math

import jax
import jax.numpy as jnp
import numpy as np
from jax import lax
from jax.experimental import pallas as pl
from jax.experimental.pallas import tpu as pltpu
from jax.sharding import PartitionSpec as P

MESH = pl.DeviceIdType.MESH
LANES = 128
ROWS = 32
FRP = 4


def gauss_nodes():
    outer = math.sqrt(5.0 + 2.0 * math.sqrt(10.0 / 7.0)) / 3.0
    inner = math.sqrt(5.0 - 2.0 * math.sqrt(10.0 / 7.0)) / 3.0
    return [-outer, -inner, 0.0, inner, outer]


def basis_value(nodes, column, x):
    value = 1.0
    for other in range(5):
        if other != column:
            value = value * (x - nodes[other]) / (nodes[column] - nodes[other])
    return value


def basis_slope(nodes, column, x):
    total = 0.0
    for skipped in range(5):
        if skipped != column:
            value = 1.0 / (nodes[column] - nodes[skipped])
            for other in range(5):
                if other != column and other != skipped:
                    value = value * (x - nodes[other]) / (nodes[column] - nodes[other])
            total = total + value
    return total


def legendre_slopes(x):
    values = [1.0, x]
    slopes = [0.0, 1.0]
    for order in range(1, 5):
        values.append(((2 * order + 1) * x * values[order] - order * values[order - 1]) / (order + 1))
        slopes.append(slopes[order - 1] + (2 * order + 1) * values[order])
    return slopes[4], slopes[5]


def split_point(p, direction):
    index = [p // 25, p // 5 % 5, p % 5]
    along = index.pop(direction)
    return along, 5 * index[0] + index[1]


def matrices():
    nodes = gauss_nodes()
    deriv = np.array([[basis_slope(nodes, m, x) for m in range(5)] for x in nodes])
    lower = np.array([basis_value(nodes, m, -1.0) for m in range(5)])
    upper = np.array([basis_value(nodes, m, 1.0) for m in range(5)])
    slopes = [legendre_slopes(x) for x in nodes]
    lift_low = np.array([-0.5 * (five - four) for four, five in slopes])
    lift_high = np.array([0.5 * (five + four) for four, five in slopes])
    folded = deriv - np.outer(lift_low, lower) - np.outer(lift_high, upper)
    faces = np.zeros((2, 3, ROWS, LANES))
    volume = np.zeros((LANES, 3, LANES))
    lift = np.zeros((LANES, 2, 3, ROWS))
    for direction in range(3):
        for p in range(125):
            i, t = split_point(p, direction)
            faces[0, direction, t, p] = upper[i]
            faces[1, direction, t, p] = lower[i]
            lift[p, 0, direction, t] = -lift_high[i]
            lift[p, 1, direction, t] = -lift_low[i]
            for other in range(125):
                m, s = split_point(other, direction)
                if s == t:
                    volume[p, direction, other] = -folded[i, m]
    faces[:, :, 25:] = faces[:, :, :1]
    return (
        jnp.asarray(faces.reshape(6 * ROWS, LANES), jnp.float32),
        jnp.asarray(volume.reshape(LANES, 3 * LANES), jnp.float32),
        jnp.asarray(lift.reshape(LANES, 6 * ROWS), jnp.float32),
    )


def lane_take(x, index):
    return jnp.take_along_axis(x, index, axis=1, mode="promise_in_bounds")


def spread(row, rows):
    return jnp.broadcast_to(row, (rows, row.shape[-1]))


def matmul(a, b):
    return jnp.dot(a, b, precision=lax.Precision.HIGH, preferred_element_type=jnp.float32)


def euler(w, direction):
    rho, momenta, energy = w[0], w[1:4], w[4]
    inverse = 1.0 / rho
    speed = momenta[direction] * inverse
    square = momenta[0] * momenta[0] + momenta[1] * momenta[1] + momenta[2] * momenta[2]
    pressure = 0.4 * (energy - 0.5 * square * inverse)
    flux = [momenta[direction]] + [m * speed for m in momenta] + [(energy + pressure) * speed]
    flux[1 + direction] = flux[1 + direction] + pressure
    return flux, speed, pressure * inverse


def common(left, right, direction):
    left_flux, left_speed, left_ratio = euler(left, direction)
    right_flux, right_speed, right_ratio = euler(right, direction)
    wave = jnp.maximum(
        jnp.abs(left_speed) + jnp.sqrt(1.4 * left_ratio),
        jnp.abs(right_speed) + jnp.sqrt(1.4 * right_ratio),
    )
    return [
        0.5 * (lf + rf) - 0.5 * wave * (r - l)
        for lf, rf, l, r in zip(left_flux, right_flux, left, right)
    ]


def load_state(state_ref, points):
    for v in range(5):
        points[v, 0:120, :] = state_ref[v, 0:120, :]
        points[v, 120:125, :] = state_ref[v, 120:125, :]
        points[v, 125:128, :] = state_ref[v, 122:125, :]


def donor_values(points, cell_ref, weight_ref, pair_weight, weight, donor_ref):
    slots = cell_ref.shape[-1]
    grids = donor_ref.shape[0]
    width = slots // grids
    weight[120:128, :] = jnp.zeros((8, slots), jnp.float32)
    for b in range(5):
        pair_weight[5 * b : 5 * b + 5, :] = weight_ref[0, 1, b : b + 1, :] * weight_ref[0, 2, :, :]
    for a in range(5):
        weight[25 * a : 25 * a + 25, :] = weight_ref[0, 0, a : a + 1, :] * pair_weight[0:25, :]
    for tile in range(slots // LANES):
        lanes = slice(tile * LANES, (tile + 1) * LANES)
        index = spread(cell_ref[0:1, lanes], LANES)
        scale = weight[:, lanes]
        for v in range(5):
            picked = lane_take(points[v], index)
            row = jnp.sum(picked * scale, axis=0, keepdims=True)
            donor_ref[tile * (LANES // width), v : v + 1, :] = row
        first = tile * (LANES // width)
        for k in range(1, LANES // width):
            donor_ref[first + k, :, :] = pltpu.roll(donor_ref[first], LANES - k * width, axis=1)


def face_slots(points, plus_ref, minus_ref, face_matrix, slot_ref):
    for v in range(5):
        faces = matmul(face_matrix, points[v])
        for side, order in ((0, plus_ref), (1, minus_ref)):
            for d in range(3):
                start = (side * 3 + d) * ROWS
                slot_ref[side, d, v] = lane_take(
                    faces[start : start + ROWS], spread(order[d : d + 1, :], ROWS)
                )


def face_messages(slot_ref, message_ref):
    count = message_ref.shape[0]
    for row in range(8):
        columns = [
            slot_ref[n // 15, n // 5 % 3, n % 5] for n in range(4 * row, min(4 * row + 4, 30))
        ]
        columns += [columns[-1]] * (4 - len(columns))
        message_ref[:, row, :] = jnp.concatenate(columns, axis=0).T[0:count]


def local_kernel(
    state_ref, plus_ref, minus_ref, cell_ref, weight_ref, face_ref,
    donor_ref, slot_ref, message_ref, points, pair_weight, weight,
):
    load_state(state_ref, points)
    donor_values(points, cell_ref, weight_ref, pair_weight, weight, donor_ref)
    face_slots(points, plus_ref, minus_ref, face_ref[...], slot_ref)
    face_messages(slot_ref, message_ref)


def ring_distance(offset, size):
    return min(offset, size - offset)


def exchange_kernel(
    grids, parts, donor_ref, message_ref, partner_ref, arrived_ref,
    gathered, relay, sends, recvs,
):
    grid = lax.axis_index("grid")
    part = lax.axis_index("dom")
    across = 4 if parts % 4 == 0 else 1
    down = parts // across

    def part_at(offset):
        z, x = offset // across, offset % across
        return lax.rem(part // across + z, down) * across + lax.rem(lax.rem(part, across) + x, across)

    grid_steps = sorted(range(1, grids), key=lambda k: -ring_distance(k, grids))
    part_steps = sorted(
        range(1, parts),
        key=lambda k: -(ring_distance(k // across, down) + ring_distance(k % across, across)),
    )
    barrier = pltpu.get_barrier_semaphore()
    for k in part_steps:
        pl.semaphore_signal(barrier, inc=1, device_id=(grid, part_at(k)), device_id_type=MESH)
    for k in grid_steps:
        pl.semaphore_signal(
            barrier, inc=1, device_id=(lax.rem(grid + k, grids), part), device_id_type=MESH
        )
    pl.semaphore_wait(barrier, grids + parts - 2)

    def to_grid(k):
        peer = lax.rem(grid + k, grids)
        return pltpu.make_async_remote_copy(
            src_ref=donor_ref.at[peer], dst_ref=gathered.at[grid],
            send_sem=sends.at[k - 1], recv_sem=recvs.at[k - 1],
            device_id=(peer, part), device_id_type=MESH,
        )

    def to_part(k, source, target, base):
        peer = part_at(k)
        return pltpu.make_async_remote_copy(
            src_ref=source.at[peer], dst_ref=target.at[part],
            send_sem=sends.at[base + k - 1], recv_sem=recvs.at[base + k - 1],
            device_id=(grid, peer), device_id_type=MESH,
        )

    first = [to_grid(k) for k in grid_steps]
    faces = [to_part(k, message_ref, partner_ref, grids - 1) for k in part_steps]
    second = [to_part(k, relay, arrived_ref, grids + parts - 2) for k in part_steps]
    for copy in first:
        copy.start()
    for copy in faces:
        copy.start()
    gathered[grid] = donor_ref[grid]
    partner_ref[part] = message_ref[part]
    for copy in first:
        copy.wait_recv()
    width = gathered.shape[2]
    turned = gathered[...].reshape(grids * 8, width)
    if grids * 8 < LANES:
        turned = jnp.concatenate([turned] * (LANES // (grids * 8)), axis=0)
    turned = turned.T
    relay[...] = turned[0 : relay.shape[0] * relay.shape[1]].reshape(relay.shape)
    for copy in second:
        copy.start()
    arrived_ref[part] = relay[part]
    for copy in faces:
        copy.wait_recv()
    for copy in second:
        copy.wait_recv()
    for copy in first + faces + second:
        copy.wait_send()


def fringe_values(arrived_ref, pick_ref, by_grid, fringe):
    parts, slots, width = arrived_ref.shape
    grids = by_grid.shape[0]
    each = parts * slots
    turned = arrived_ref[...].reshape(each, width)
    turned = jnp.concatenate([turned] * (LANES // each), axis=0).T
    by_grid[...] = turned[0 : grids * 8].reshape(grids, 8, LANES)
    for k in range(6):
        pick = spread(pick_ref[k : k + 1, :], 8)
        owner, place = pick // each, lax.rem(pick, each)
        value = lane_take(by_grid[0], place)
        for g in range(1, grids):
            value = jnp.where(owner == g, lane_take(by_grid[g], place), value)
        fringe[k] = value


def finish_kernel(
    remote, state_ref, scale_ref, plus_ref, minus_ref, pick_ref, slot_ref, partner_ref, arrived_ref,
    volume_ref, lift_ref, out_ref, points, by_grid, fringe, partner, flux, jump,
):
    load_state(state_ref, points)
    w = [points[v] for v in range(5)]
    for d in range(3):
        pieces = euler(w, d)[0]
        for v in range(5):
            flux[v, d * LANES : (d + 1) * LANES, :] = pieces[v] * spread(scale_ref[d : d + 1, :], LANES)

    for row in range(8):
        block = partner_ref[:, row, :]
        block = jnp.concatenate([block] * (LANES // remote), axis=0).T
        partner[row * LANES : (row + 1) * LANES, :] = block
    fringe_values(arrived_ref, pick_ref, by_grid, fringe)

    lane = lax.broadcasted_iota(jnp.int32, (ROWS, LANES), 1)
    point = lax.broadcasted_iota(jnp.int32, (ROWS, LANES), 0)
    point = jnp.where(point < 25, point, 0)
    place = jnp.clip(FRP * point + lane - remote, 0, LANES - 1)
    shared, outer = lane < remote, lane < remote + FRP
    element = lax.broadcasted_iota(jnp.int32, (LANES, LANES), 0)
    count = lax.broadcasted_iota(jnp.int32, (8, LANES), 1).astype(jnp.bfloat16)

    def inverse(order):
        chosen = (element == spread(order, LANES)).astype(jnp.float32).astype(jnp.bfloat16)
        slots = lax.dot_general(
            count, chosen, (((1,), (1,)), ((), ())), preferred_element_type=jnp.float32
        )
        return spread(slots[0:1].astype(jnp.int32), ROWS)

    def other(side, d, v, own):
        start = ((side * 3 + d) * 5 + v) * ROWS
        edge = lane_take(spread(fringe[2 * d + side, v : v + 1, :], ROWS), place)
        return jnp.where(shared, partner[start : start + ROWS, :], jnp.where(outer, edge, own))

    for d in range(3):
        high = [slot_ref[0, d, v] for v in range(5)]
        low = [slot_ref[1, d, v] for v in range(5)]
        right = [other(1, d, v, low[v]) for v in range(5)]
        left = [other(0, d, v, high[v]) for v in range(5)]
        scale = spread(scale_ref[d : d + 1, :], ROWS)
        for side, order, value in (
            (0, plus_ref, common(high, right, d)),
            (1, minus_ref, common(left, low, d)),
        ):
            back = inverse(order[d : d + 1, :])
            start = (side * 3 + d) * ROWS
            for v in range(5):
                jump[v, start : start + ROWS, :] = lane_take(value[v], back) * scale
    for v in range(5):
        total = matmul(volume_ref[...], flux[v]) + matmul(lift_ref[...], jump[v])
        out_ref[v] = total[0:125]


def body(grids, parts, state, scales, plus, minus, cell, weights, picks):
    vmem = pl.BlockSpec(memory_space=pltpu.VMEM)
    f32 = jnp.float32
    slots = cell.shape[-1] // (grids * parts)
    face_matrix, volume, lift = matrices()
    donors, own, messages = pl.pallas_call(
        local_kernel,
        out_shape=(
            jax.ShapeDtypeStruct((grids, 8, LANES), f32),
            jax.ShapeDtypeStruct((2, 3, 5, ROWS, LANES), f32),
            jax.ShapeDtypeStruct((parts, 8, LANES), f32),
        ),
        in_specs=[vmem] * 6,
        out_specs=(vmem,) * 3,
        scratch_shapes=[
            pltpu.VMEM((5, LANES, LANES), f32),
            pltpu.VMEM((32, cell.shape[-1]), f32),
            pltpu.VMEM((LANES, cell.shape[-1]), f32),
        ],
        name="local",
    )(state, plus, minus, cell, weights, face_matrix)

    copies = grids - 1 + 2 * (parts - 1)
    partner, arrived = pl.pallas_call(
        functools.partial(exchange_kernel, grids, parts),
        out_shape=(
            jax.ShapeDtypeStruct((parts, 8, LANES), f32),
            jax.ShapeDtypeStruct((parts, slots, LANES), f32),
        ),
        in_specs=[vmem] * 2,
        out_specs=(vmem,) * 2,
        scratch_shapes=[
            pltpu.VMEM((grids, 8, LANES), f32),
            pltpu.VMEM((parts, slots, LANES), f32),
            pltpu.SemaphoreType.DMA((copies,)),
            pltpu.SemaphoreType.DMA((copies,)),
        ],
        compiler_params=pltpu.CompilerParams(collective_id=0, has_side_effects=True),
        name="exchange",
    )(donors, messages)

    picks = jnp.pad(picks.reshape(6, 25 * FRP), ((0, 0), (0, LANES - 25 * FRP)))
    return pl.pallas_call(
        functools.partial(finish_kernel, parts),
        out_shape=jax.ShapeDtypeStruct(state.shape, f32),
        in_specs=[vmem] * 10,
        out_specs=vmem,
        scratch_shapes=[
            pltpu.VMEM((5, LANES, LANES), f32),
            pltpu.VMEM((grids, 8, LANES), f32),
            pltpu.VMEM((6, 8, LANES), f32),
            pltpu.VMEM((8 * LANES, LANES), f32),
            pltpu.VMEM((5, 3 * LANES, LANES), f32),
            pltpu.VMEM((5, 6 * ROWS, LANES), f32),
        ],
        name="finish",
    )(state, scales, plus, minus, picks, own, partner, arrived, volume, lift)


def solution(mesh):
    both = ("grid", "dom")
    return jax.shard_map(
        functools.partial(body, mesh.shape["grid"], mesh.shape["dom"]),
        mesh=mesh,
        in_specs=(
            P(None, None, both),
            P(None, both),
            P(None, both),
            P(None, both),
            P(both, None),
            P(both, None, None, None),
            P(both, None),
        ),
        out_specs=P(None, None, both),
        check_vma=False,
    )
```

time: 258 us -> 39.5 us (0.15); the launches traced: 254 us -> 39.2 us
  local copies, waits for them, and re-layouts: 120 us -> 2.15 us
  other arithmetic: 60 us -> 0.7 us
  starting transfers between devices: 36.7 us -> 0 us
  Pallas kernels: 0 us -> 36.4 us
  matrix products: 15.5 us -> 0 us
  loops' own time: 10.8 us -> 0 us
  waiting for transfers between devices: 8.82 us -> 0 us
    unnamed x296 -> x1, local copies, waits for them, and re-layouts: 47.7 us -> 1.48 us
    all_to_all x4 -> x0, starting transfers between devices: 36.7 us -> none  [the longest x1 11.3 us: body(): lax.all_to_all(lax.all_to_all(shaped, 'grid', split_axis=1, concat_axis=1...]
    pallas_call x0 -> x3, Pallas kernels: none -> 36.4 us  [the longest x1 29.1 us: body(): pl.pallas_call(functools.partial(exchange_kernel, grids, parts), out_shap...]
    gather x62 -> x0, local copies, waits for them, and re-layouts: 29.2 us -> none  [the longest x48 14.1 us: one_block(): jnp.take(state, block_cells, axis=2).reshape(5, 5, 5, 5, block_width)]
    and x25 -> x0, other arithmetic: 16.8 us -> none  [the longest x16 12.3 us: one_block(): jnp.take(state, block_cells, axis=2).reshape(5, 5, 5, 5, block_width)]
    dot_general x15 -> x0, matrix products: 15.5 us -> none  [the longest x3 3.66 us: divergence(): inner = jnp.einsum(volume_forms[direction], deriv, flux, precision=precise)]
    another operation x1 -> x0, loops' own time: 10.8 us -> none  [interpolate(): values = lax.map(one_block, jnp.arange(blocks, dtype=jnp.int32))]
    reduce_sum x18 -> x0, other arithmetic: 10.1 us -> none  [euler_flux(): jnp.sum(momenta * momenta, axis=0)]
  transfers between devices with their start and end apart: 4 -> 0, of which waited for: 2 -> 0; matrix products, arithmetic and copies ran while one was open for 34% -> 0% of each run, Pallas kernels for 0% -> 0%
where the time goes in v1:
time: 39.5 us; the launch traced here: 39.2 us
  Pallas kernels  36.4 us (92%)
  local copies, waits for them, and re-layouts  2.15 us (5%)
  other arithmetic  0.7 us (2%)
    pallas_call x1, Pallas kernels, body(): pl.pallas_call(functools.partial(exchange_kernel, grids, parts), out_shap...  29.1 us
    pallas_call x1, Pallas kernels, body(): pl.pallas_call(functools.partial(finish_kernel, parts), out_shape=jax.Sha...  3.75 us
    pallas_call x1, Pallas kernels, body(): pl.pallas_call(local_kernel, out_shape=(jax.ShapeDtypeStruct((grids, 8, L...  3.48 us
    unnamed x1, local copies, waits for them, and re-layouts  1.48 us

profile of v1, /device:TPU:1, one launch (start us, length us, event | category | flops | bytes accessed | tf_op | source)
XLA Modules:
  0.0 39.2 jit_solution(2734614430374784871)
XLA Ops:
  0.0 0.7 %reduce = s32[600]{0:T(1024)S(1)} reduce(s32[1,600]{1,0:T(1,128)} %param.16, s32[]{:T(128)} %constant.3.clone.1), dimensions={0}, to_apply=%param.16.reduce_sub_computation | reduce | bytes 4804 | tf_op args[6]
  0.7 0.1 reshape.3
  0.8 0.6 %pad.4.pick_ref = s32[6,128]{1,0:T(8,128)} pad(s32[6,100]{1,0:T(8,128)S(1)} %reshape.3, s32[]{:T(128)} %constant.3.clone.1), padding=0_0x0_28 | pad | bytes 5476 | tf_op jit(solution)/shard_map/jit(_pad)/pad | solution.py:374
  1.4 1.5 %copy.11.weight_ref = f32[1,3,5,1024]{3,2,1,0:T(8,128)} copy(f32[1,3,5,1024]{3,0,2,1:T(1,128)} %param.15) | data formatting | bytes 122880 | tf_op args[5]
  2.9 3.5 %local.1 = (f32[16,8,128]{2,1,0:T(8,128)}, f32[2,3,5,32,128]{4,3,2,1,0:T(8,128)}, f32[32,8,128]{2,1,0:T(8,128)}) custom-call(f32[5,125,128]{2,1,0:T(8,128)} %state_ref.3, s32[3,128]{1,0:T(4,128)} %plus_ref.3, s32[3,128]{1,0:T(4,128)} %minus_ref.3, s32[1,1024]{1,0:T(1,128)} %cell_ref.1, f32[1,3,5,1024]{3,2,1,0:T(8,128)} %copy.11.weight_ref, ...), custom_call_target="tpu_custom_call" | custom-call | tf_op jit(solution)/shard_map/local/pallas_call | solution.py:338
  6.3 29.1 %exchange.1 = (f32[32,8,128]{2,1,0:T(8,128)}, f32[32,2,128]{2,1,0:T(2,128)}) custom-call(f32[16,8,128]{2,1,0:T(8,128)} %get-tuple-element.11.donor_ref, f32[32,8,128]{2,1,0:T(8,128)} %get-tuple-element.12.message_ref), custom_call_target="tpu_custom_call" | custom-call | tf_op jit(solution)/shard_map/exchange/pallas_call | solution.py:356
  35.5 3.8 %finish.1 = f32[5,125,128]{2,1,0:T(8,128)} custom-call(f32[5,125,128]{2,1,0:T(8,128)} %state_ref.3, f32[3,128]{1,0:T(4,128)} %scale_ref.1, s32[3,128]{1,0:T(4,128)} %plus_ref.3, s32[3,128]{1,0:T(4,128)} %minus_ref.3, s32[6,128]{1,0:T(8,128)} %pad.4.pick_ref, f32[2,3,5,32,128]{4,3,2,1,0:T(8,128)} %get-tuple-element.10.slot_ref, ...), custom_call_target="tpu_custom_call" | custom-call | tf_op jit(solution)/shard_map/finish/pallas_call | solution.py:375

commit v2 on v1

v2 whole, which is shorter than its diff:
```python
import functools
import math

import jax
import jax.numpy as jnp
import numpy as np
from jax import lax
from jax.experimental import pallas as pl
from jax.experimental.pallas import tpu as pltpu
from jax.sharding import PartitionSpec as P

MESH = pl.DeviceIdType.MESH
LANES = 128
ROWS = 32
FRP = 4


def gauss_nodes():
    outer = math.sqrt(5.0 + 2.0 * math.sqrt(10.0 / 7.0)) / 3.0
    inner = math.sqrt(5.0 - 2.0 * math.sqrt(10.0 / 7.0)) / 3.0
    return [-outer, -inner, 0.0, inner, outer]


def basis_value(nodes, column, x):
    value = 1.0
    for other in range(5):
        if other != column:
            value = value * (x - nodes[other]) / (nodes[column] - nodes[other])
    return value


def basis_slope(nodes, column, x):
    total = 0.0
    for skipped in range(5):
        if skipped != column:
            value = 1.0 / (nodes[column] - nodes[skipped])
            for other in range(5):
                if other != column and other != skipped:
                    value = value * (x - nodes[other]) / (nodes[column] - nodes[other])
            total = total + value
    return total


def legendre_slopes(x):
    values = [1.0, x]
    slopes = [0.0, 1.0]
    for order in range(1, 5):
        values.append(((2 * order + 1) * x * values[order] - order * values[order - 1]) / (order + 1))
        slopes.append(slopes[order - 1] + (2 * order + 1) * values[order])
    return slopes[4], slopes[5]


def split_point(p, direction):
    index = [p // 25, p // 5 % 5, p % 5]
    along = index.pop(direction)
    return along, 5 * index[0] + index[1]


def matrices():
    nodes = gauss_nodes()
    deriv = np.array([[basis_slope(nodes, m, x) for m in range(5)] for x in nodes])
    lower = np.array([basis_value(nodes, m, -1.0) for m in range(5)])
    upper = np.array([basis_value(nodes, m, 1.0) for m in range(5)])
    slopes = [legendre_slopes(x) for x in nodes]
    lift_low = np.array([-0.5 * (five - four) for four, five in slopes])
    lift_high = np.array([0.5 * (five + four) for four, five in slopes])
    folded = deriv - np.outer(lift_low, lower) - np.outer(lift_high, upper)
    faces = np.zeros((2, 3, ROWS, LANES))
    volume = np.zeros((LANES, 3, LANES))
    lift = np.zeros((LANES, 2, 3, ROWS))
    for direction in range(3):
        for p in range(125):
            i, t = split_point(p, direction)
            faces[0, direction, t, p] = upper[i]
            faces[1, direction, t, p] = lower[i]
            lift[p, 0, direction, t] = -lift_high[i]
            lift[p, 1, direction, t] = -lift_low[i]
            for other in range(125):
                m, s = split_point(other, direction)
                if s == t:
                    volume[p, direction, other] = -folded[i, m]
    faces[:, :, 25:] = faces[:, :, :1]
    return (
        jnp.asarray(faces.reshape(6 * ROWS, LANES), jnp.float32),
        jnp.asarray(volume.reshape(LANES, 3 * LANES), jnp.float32),
        jnp.asarray(lift.reshape(LANES, 6 * ROWS), jnp.float32),
    )


def lane_take(x, index):
    return jnp.take_along_axis(x, index, axis=1, mode="promise_in_bounds")


def spread(row, rows):
    return jnp.broadcast_to(row, (rows, row.shape[-1]))


def matmul(a, b):
    return jnp.dot(a, b, precision=lax.Precision.HIGH, preferred_element_type=jnp.float32)


def pressure_of(w, inverse):
    square = w[1] * w[1] + w[2] * w[2] + w[3] * w[3]
    return 0.4 * (w[4] - 0.5 * square * inverse)


def euler(w, direction):
    inverse = 1.0 / w[0]
    speed = w[1 + direction] * inverse
    pressure = pressure_of(w, inverse)
    flux = [w[1 + direction]] + [m * speed for m in w[1:4]] + [(w[4] + pressure) * speed]
    flux[1 + direction] = flux[1 + direction] + (pressure - 1.0)
    return flux, jnp.abs(speed) + jnp.sqrt(1.4 * pressure * inverse)


def common(left, right, direction):
    left_flux, left_wave = euler(left, direction)
    right_flux, right_wave = euler(right, direction)
    wave = jnp.maximum(left_wave, right_wave)
    return [
        0.5 * (lf + rf) - 0.5 * wave * (r - l)
        for lf, rf, l, r in zip(left_flux, right_flux, left, right)
    ]


def lane_euler(w, normal):
    inverse = 1.0 / w[0]
    momentum = jnp.where(normal[0], w[1], jnp.where(normal[1], w[2], w[3]))
    speed = momentum * inverse
    pressure = pressure_of(w, inverse)
    flux = [momentum] + [
        w[1 + d] * speed + jnp.where(normal[d], pressure - 1.0, 0.0) for d in range(3)
    ]
    flux.append((w[4] + pressure) * speed)
    return flux, jnp.abs(speed) + jnp.sqrt(1.4 * pressure * inverse)


def load_state(state_ref, points):
    for v in range(5):
        points[v, 0:120, :] = state_ref[v, 0:120, :]
        points[v, 120:125, :] = state_ref[v, 120:125, :]
        points[v, 125:128, :] = state_ref[v, 122:125, :]


def donor_values(points, cell_ref, weight_ref, pair_weight, weight, donor_ref):
    slots = cell_ref.shape[-1]
    grids = donor_ref.shape[0]
    width = slots // grids
    weight[120:128, :] = jnp.zeros((8, slots), jnp.float32)
    for b in range(5):
        for c in range(5):
            row = 5 * b + c
            pair_weight[row : row + 1, :] = weight_ref[1, b] * weight_ref[2, c]
    for a in range(5):
        weight[25 * a : 25 * a + 25, :] = weight_ref[0, a] * pair_weight[0:25, :]
    for tile in range(slots // LANES):
        lanes = slice(tile * LANES, (tile + 1) * LANES)
        index = spread(cell_ref[0:1, lanes], LANES)
        scale = weight[:, lanes]
        first = tile * (LANES // width)
        for v in range(5):
            picked = lane_take(points[v], index)
            donor_ref[first, v : v + 1, :] = jnp.sum(picked * scale, axis=0, keepdims=True)
        for k in range(1, LANES // width):
            donor_ref[first + k, :, :] = pltpu.roll(donor_ref[first], LANES - k * width, axis=1)


def face_slots(points, plus_ref, minus_ref, face_matrix, slot_ref):
    for v in range(5):
        centre = (1.0, 0.0, 0.0, 0.0, 2.5)[v]
        faces = matmul(face_matrix, points[v] - centre) + centre
        for side, order in ((0, plus_ref), (1, minus_ref)):
            for d in range(3):
                start = (side * 3 + d) * ROWS
                slot_ref[side, d, v] = lane_take(
                    faces[start : start + ROWS], spread(order[d : d + 1, :], ROWS)
                )


def face_messages(slot_ref, message_ref):
    count = message_ref.shape[0]
    for row in range(8):
        columns = [
            slot_ref[n // 15, n // 5 % 3, n % 5] for n in range(4 * row, min(4 * row + 4, 30))
        ]
        columns += [columns[-1]] * (4 - len(columns))
        message_ref[:, row, :] = jnp.concatenate(columns, axis=0).T[0:count]


def volume_terms(points, scale_ref, volume_ref, flux, total):
    w = [points[v] for v in range(5)]
    for d in range(3):
        pieces = euler(w, d)[0]
        for v in range(5):
            flux[v, d * LANES : (d + 1) * LANES, :] = pieces[v] * spread(scale_ref[d : d + 1, :], LANES)
    for v in range(5):
        total[v] = matmul(volume_ref[...], flux[v])


def inverse_orders(plus_ref, minus_ref, inverse):
    element = lax.broadcasted_iota(jnp.int32, (LANES, LANES), 0)
    count = lax.broadcasted_iota(jnp.int32, (8, LANES), 1).astype(jnp.float32).astype(jnp.bfloat16)
    for side, order in ((0, plus_ref), (1, minus_ref)):
        for d in range(3):
            chosen = element == spread(order[d : d + 1, :], LANES)
            chosen = jnp.where(chosen, 1.0, 0.0).astype(jnp.bfloat16)
            inverse[side * 3 + d] = lax.dot_general(
                count, chosen, (((1,), (1,)), ((), ())), preferred_element_type=jnp.float32
            ).astype(jnp.int32)


def fringe_picks(pick_ref, pick_rows, pick):
    pick_rows[...] = jnp.zeros(pick_rows.shape, jnp.int32)
    pick_rows[0:1, 0 : pick_ref.shape[1]] = pick_ref[...]
    row = lax.broadcasted_iota(jnp.int32, (8, LANES), 0)
    lane = lax.broadcasted_iota(jnp.int32, (8, LANES), 1)
    block, face = lane // 24, lane // 4 - 6 * (lane // 24)
    side, d = face // 3, face - 3 * (face // 3)
    t = jnp.minimum(8 * block + row, 24)
    number = ((2 * d + 1 - side) * 25 + t) * FRP + lane - 4 * (lane // 4)
    tile, place = number // LANES, number - LANES * (number // LANES)
    value = jnp.zeros((8, LANES), jnp.int32)
    for k in range(pick_rows.shape[1] // LANES):
        source = spread(pick_rows[0:1, k * LANES : (k + 1) * LANES], 8)
        value = jnp.where(tile == k, lane_take(source, place), value)
    pick[...] = value


def fringe_own(slot_ref, remote, own):
    lane = lax.broadcasted_iota(jnp.int32, (8, LANES), 1)
    for v in range(5):
        value = slot_ref[0, 0, v, 0:8, :]
        for k in range(6):
            for block in range(4):
                start = 24 * block + 4 * k
                source = slot_ref[k // 3, k % 3, v, 8 * block : 8 * block + 8, :]
                source = pltpu.roll(source, (start - remote) % LANES, axis=1)
                value = jnp.where((lane >= start) & (lane < start + 4), source, value)
        own[v] = value


def inner_jumps(remote, slot_ref, partner, scale_ref, inverse, jump):
    shared = lax.broadcasted_iota(jnp.int32, (ROWS, LANES), 1) < remote
    for d in range(3):
        high = [slot_ref[0, d, v] for v in range(5)]
        low = [slot_ref[1, d, v] for v in range(5)]

        def other(side, own):
            starts = [((side * 3 + d) * 5 + v) * ROWS for v in range(5)]
            return [jnp.where(shared, partner[s : s + ROWS, :], o) for s, o in zip(starts, own)]

        scale = spread(scale_ref[d : d + 1, :], ROWS)
        for side, value in (
            (0, common(high, other(1, low), d)),
            (1, common(other(0, high), low, d)),
        ):
            back = jnp.concatenate([inverse[side * 3 + d]] * 4, axis=0)
            start = (side * 3 + d) * ROWS
            for v in range(5):
                jump[v, start : start + ROWS, :] = lane_take(value[v], back) * scale


def fringe_jumps(remote, arrived_ref, pick, own, by_grid, scale_ref, inverse, jump):
    parts, slots, width = arrived_ref.shape
    grids = by_grid.shape[0]
    each = parts * slots
    turned = arrived_ref[...].reshape(each, width)
    turned = jnp.concatenate([turned] * (LANES // each), axis=0).T
    by_grid[...] = turned[0 : grids * 8].reshape(grids, 8, LANES)
    chosen = pick[...]
    owner, place = chosen // each, chosen - each * (chosen // each)
    outside = []
    for v in range(5):
        value = lane_take(spread(by_grid[0, v : v + 1, :], 8), place)
        for g in range(1, grids):
            source = lane_take(spread(by_grid[g, v : v + 1, :], 8), place)
            value = jnp.where(owner == g, source, value)
        outside.append(value)
    inside = [own[v] for v in range(5)]
    lane = lax.broadcasted_iota(jnp.int32, (8, LANES), 1)
    face = lane // 4 - 6 * (lane // 24)
    d = face - 3 * (face // 3)
    normal = [d == n for n in range(3)]
    sign = jnp.where(face < 3, 0.5, -0.5)
    outer_flux, outer_wave = lane_euler(outside, normal)
    inner_flux, inner_wave = lane_euler(inside, normal)
    wave = sign * jnp.maximum(outer_wave, inner_wave)
    value = [
        0.5 * (a + b) - wave * (o - i)
        for a, b, o, i in zip(outer_flux, inner_flux, outside, inside)
    ]
    for k in range(6):
        slot = inverse[k] - remote
        here = (slot >= 0) & (slot < FRP)
        slot = jnp.where(here, slot, 0) + 4 * k
        scale = spread(scale_ref[k % 3 : k % 3 + 1, :], 8)
        for block in range(4):
            rows = slice(k * ROWS + 8 * block, k * ROWS + 8 * block + 8)
            for v in range(5):
                new = lane_take(value[v], slot + 24 * block) * scale
                jump[v, rows, :] = jnp.where(here, new, jump[v, rows, :])


def ring_distance(offset, size):
    return min(offset, size - offset)


def kernel(grids, parts, *refs):
    inputs, (out_ref,), buffers, scratch = refs[:10], refs[10:11], refs[11:21], refs[21:]
    (state_ref, scale_ref, plus_ref, minus_ref, cell_ref, weight_ref, pick_ref) = buffers[:7]
    face_ref, volume_ref, lift_ref = buffers[7:]
    (
        points, pair_weight, weight, donor, slot, message, partner_in, gathered, relay, arrived,
        flux, total, inverse, pick_rows, pick, own, partner, jump, by_grid,
        load_sem, sends, recvs,
    ) = scratch
    grid = lax.axis_index("grid")
    part = lax.axis_index("dom")
    across = 4 if parts % 4 == 0 else 1
    down = parts // across

    def part_at(offset):
        z, x = offset // across, offset % across
        return lax.rem(part // across + z, down) * across + lax.rem(lax.rem(part, across) + x, across)

    grid_steps = sorted(range(1, grids), key=lambda k: -ring_distance(k, grids))
    part_steps = sorted(
        range(1, parts),
        key=lambda k: -(ring_distance(k // across, down) + ring_distance(k % across, across)),
    )
    barrier = pltpu.get_barrier_semaphore()
    for k in part_steps:
        pl.semaphore_signal(barrier, inc=1, device_id=(grid, part_at(k)), device_id_type=MESH)
    for k in grid_steps:
        pl.semaphore_signal(
            barrier, inc=1, device_id=(lax.rem(grid + k, grids), part), device_id_type=MESH
        )
    loads = [
        pltpu.make_async_copy(source, target, load_sem.at[n])
        for n, (source, target) in enumerate(zip(inputs, buffers))
    ]
    for n in (0, 4, 5, 2, 3, 7, 1, 6, 8, 9):
        loads[n].start()

    def to_grid(k):
        peer = lax.rem(grid + k, grids)
        return pltpu.make_async_remote_copy(
            src_ref=donor.at[peer], dst_ref=gathered.at[grid],
            send_sem=sends.at[k - 1], recv_sem=recvs.at[k - 1],
            device_id=(peer, part), device_id_type=MESH,
        )

    def to_part(k, source, target, base):
        peer = part_at(k)
        return pltpu.make_async_remote_copy(
            src_ref=source.at[peer], dst_ref=target.at[part],
            send_sem=sends.at[base + k - 1], recv_sem=recvs.at[base + k - 1],
            device_id=(grid, peer), device_id_type=MESH,
        )

    first = [to_grid(k) for k in grid_steps]
    faces = [to_part(k, message, partner_in, grids - 1) for k in part_steps]
    second = [to_part(k, relay, arrived, grids + parts - 2) for k in part_steps]

    loads[0].wait()
    load_state(state_ref, points)
    loads[4].wait()
    loads[5].wait()
    donor_values(points, cell_ref, weight_ref, pair_weight, weight, donor)
    for n in (2, 3, 7):
        loads[n].wait()
    face_slots(points, plus_ref, minus_ref, face_ref[...], slot)
    face_messages(slot, message)

    pl.semaphore_wait(barrier, grids + parts - 2)
    for copy in first:
        copy.start()
    for copy in faces:
        copy.start()
    gathered[grid] = donor[grid]
    partner_in[part] = message[part]

    for n in (1, 6, 8, 9):
        loads[n].wait()
    volume_terms(points, scale_ref, volume_ref, flux, total)
    inverse_orders(plus_ref, minus_ref, inverse)
    fringe_picks(pick_ref, pick_rows, pick)
    fringe_own(slot, parts, own)

    for copy in first:
        copy.wait_recv()
    turned = gathered[...].reshape(grids * 8, LANES)
    if grids * 8 < LANES:
        turned = jnp.concatenate([turned] * (LANES // (grids * 8)), axis=0)
    relay[...] = turned.T[0 : relay.shape[0] * relay.shape[1]].reshape(relay.shape)
    for copy in second:
        copy.start()
    arrived[part] = relay[part]

    for copy in faces:
        copy.wait_recv()
    for row in range(8):
        block = partner_in[:, row, :]
        block = jnp.concatenate([block] * (LANES // parts), axis=0).T
        partner[row * LANES : (row + 1) * LANES, :] = block
    inner_jumps(parts, slot, partner, scale_ref, inverse, jump)

    for copy in second:
        copy.wait_recv()
    fringe_jumps(parts, arrived, pick, own, by_grid, scale_ref, inverse, jump)
    for v in range(5):
        value = total[v] + matmul(lift_ref[...], jump[v])
        out_ref[v] = value[0:125]
    for copy in first + faces + second:
        copy.wait_send()


def body(grids, parts, state, scales, plus, minus, cell, weights, picks):
    f32, i32 = jnp.float32, jnp.int32
    total_slots = cell.shape[-1]
    slots = total_slots // (grids * parts)
    weights = jnp.transpose(weights, (1, 2, 0, 3))
    inputs = (state, scales, plus, minus, cell, weights, picks) + matrices()
    copies = grids - 1 + 2 * (parts - 1)
    pick_tiles = -(-picks.shape[-1] // LANES)
    return pl.pallas_call(
        functools.partial(kernel, grids, parts),
        out_shape=jax.ShapeDtypeStruct(state.shape, f32),
        in_specs=[pl.BlockSpec(memory_space=pl.ANY)] * len(inputs),
        out_specs=pl.BlockSpec(memory_space=pltpu.VMEM),
        scratch_shapes=[pltpu.VMEM(x.shape, x.dtype) for x in inputs]
        + [
            pltpu.VMEM((5, LANES, LANES), f32),
            pltpu.VMEM((32, total_slots), f32),
            pltpu.VMEM((LANES, total_slots), f32),
            pltpu.VMEM((grids, 8, LANES), f32),
            pltpu.VMEM((2, 3, 5, ROWS, LANES), f32),
            pltpu.VMEM((parts, 8, LANES), f32),
            pltpu.VMEM((parts, 8, LANES), f32),
            pltpu.VMEM((grids, 8, LANES), f32),
            pltpu.VMEM((parts, slots, LANES), f32),
            pltpu.VMEM((parts, slots, LANES), f32),
            pltpu.VMEM((5, 3 * LANES, LANES), f32),
            pltpu.VMEM((5, LANES, LANES), f32),
            pltpu.VMEM((6, 8, LANES), i32),
            pltpu.VMEM((8, pick_tiles * LANES), i32),
            pltpu.VMEM((8, LANES), i32),
            pltpu.VMEM((5, 8, LANES), f32),
            pltpu.VMEM((8 * LANES, LANES), f32),
            pltpu.VMEM((5, 6 * ROWS, LANES), f32),
            pltpu.VMEM((grids, 8, LANES), f32),
            pltpu.SemaphoreType.DMA((len(inputs),)),
            pltpu.SemaphoreType.DMA((copies,)),
            pltpu.SemaphoreType.DMA((copies,)),
        ],
        compiler_params=pltpu.CompilerParams(collective_id=0, has_side_effects=True),
        name="step",
    )(*inputs)


def solution(mesh):
    both = ("grid", "dom")
    return jax.shard_map(
        functools.partial(body, mesh.shape["grid"], mesh.shape["dom"]),
        mesh=mesh,
        in_specs=(
            P(None, None, both),
            P(None, both),
            P(None, both),
            P(None, both),
            P(both, None),
            P(both, None, None, None),
            P(both, None),
        ),
        out_specs=P(None, None, both),
        check_vma=False,
    )
```

time: 39.5 us -> 31.2 us (0.79)
  Pallas kernels: 36.4 us -> 29.3 us
  other arithmetic: 0.7 us -> 0 us
  local copies, waits for them, and re-layouts: 2.15 us -> 1.72 us
    pallas_call x3 -> x1, Pallas kernels: 36.4 us -> 29.3 us  [body(): pl.pallas_call(functools.partial(kernel, grids, parts), out_shape=jax.Sha...]
    unnamed x1 -> x0, other arithmetic: 0.7 us -> none
    pad x1 -> x0, local copies, waits for them, and re-layouts: 0.6 us -> none  [body(): picks = jnp.pad(picks.reshape(6, 25 * FRP), ((0, 0), (0, LANES - 25 * FRP)))]
where the time goes in v2:
time: 31.2 us; the launch traced here: 31.1 us
  Pallas kernels  29.3 us (94%)
  local copies, waits for them, and re-layouts  1.72 us (6%)
    pallas_call x1, Pallas kernels, body(): pl.pallas_call(functools.partial(kernel, grids, parts), out_shape=jax.Sha...  29.3 us
    unnamed x1, local copies, waits for them, and re-layouts  1.72 us

profile of v2, /device:TPU:1, one launch (start us, length us, event | category | flops | bytes accessed | tf_op | source)
XLA Modules:
  0.0 31.1 jit_solution(2748541341798131520)
XLA Ops:
  0.0 29.3 %step.1 = f32[5,125,128]{2,1,0:T(8,128)} custom-call(f32[5,125,128]{2,1,0:T(8,128)} %refs_0_.1, f32[3,128]{1,0:T(4,128)} %refs_1_.1, s32[3,128]{1,0:T(4,128)} %refs_2_.1, s32[3,128]{1,0:T(4,128)} %refs_3_.1, s32[1,1024]{1,0:T(1,128)} %refs_4_.1, f32[3,5,1,1024]{3,2,1,0:T(1,128)} %bitcast.1, s32[1,600]{1,0:T(1,128)} %refs_6_.1, ...), custom_call_target="tpu_custom_call" | custom-call | tf_op jit(solution)/shard_map/step/pallas_call | solution.py:426
  29.4 1.7 %copy.12 = f32[5,125,128]{2,1,0:T(8,128)} copy(f32[5,125,128]{2,1,0:T(8,128)} %step.1) | data formatting | bytes 640000

commit v3 on v2

--- a/solution.py
+++ b/solution.py
@@ -54,6 +54,12 @@
     index = [p // 25, p // 5 % 5, p % 5]
     along = index.pop(direction)
     return along, 5 * index[0] + index[1]
+
+
+def split_constant(matrix):
+    high = matrix.astype(jnp.bfloat16)
+    low = (matrix - high.astype(np.float32)).astype(jnp.bfloat16)
+    return jnp.asarray(np.concatenate([high, high, low], axis=1))
 
 
 def matrices():
@@ -80,10 +86,13 @@
                 if s == t:
                     volume[p, direction, other] = -folded[i, m]
     faces[:, :, 25:] = faces[:, :, :1]
-    return (
-        jnp.asarray(faces.reshape(6 * ROWS, LANES), jnp.float32),
-        jnp.asarray(volume.reshape(LANES, 3 * LANES), jnp.float32),
-        jnp.asarray(lift.reshape(LANES, 6 * ROWS), jnp.float32),
+    return tuple(
+        split_constant(m.astype(np.float32))
+        for m in (
+            faces.reshape(6 * ROWS, LANES),
+            volume.reshape(LANES, 3 * LANES),
+            lift.reshape(LANES, 6 * ROWS),
+        )
     )
 
 
@@ -95,8 +104,23 @@
     return jnp.broadcast_to(row, (rows, row.shape[-1]))
 
 
-def matmul(a, b):
-    return jnp.dot(a, b, precision=lax.Precision.HIGH, preferred_element_type=jnp.float32)
+def store_parts(ref, start, v, value):
+    third = ref.shape[0] // 3
+    rows, lanes = value.shape[0], slice(v * LANES, (v + 1) * LANES)
+    high = value.astype(jnp.bfloat16)
+    ref[start : start + rows, lanes] = high
+    ref[third + start : third + start + rows, lanes] = (value - high.astype(jnp.float32)).astype(jnp.bfloat16)
+    ref[2 * third + start : 2 * third + start + rows, lanes] = high
+
+
+def products(constant_ref, ref):
+    for v in range(0, 5, 2):
+        width = min(2, 5 - v) * LANES
+        block = jnp.dot(
+            constant_ref[...], ref[:, v * LANES : v * LANES + width], preferred_element_type=jnp.float32
+        )
+        for k in range(width // LANES):
+            yield v + k, block[:, k * LANES : (k + 1) * LANES]
 
 
 def pressure_of(w, inverse):
@@ -153,38 +177,54 @@
             pair_weight[row : row + 1, :] = weight_ref[1, b] * weight_ref[2, c]
     for a in range(5):
         weight[25 * a : 25 * a + 25, :] = weight_ref[0, a] * pair_weight[0:25, :]
+    row = lax.broadcasted_iota(jnp.int32, (8, LANES), 0)
     for tile in range(slots // LANES):
         lanes = slice(tile * LANES, (tile + 1) * LANES)
-        index = spread(cell_ref[0:1, lanes], LANES)
-        scale = weight[:, lanes]
+        index = spread(cell_ref[0:1, lanes], 8)
+        sums = [None] * 5
+        for k in range(LANES // 8):
+            scale = weight[8 * k : 8 * k + 8, lanes]
+            for v in range(5):
+                term = lane_take(points[v, 8 * k : 8 * k + 8, :], index) * scale
+                sums[v] = term if k == 0 else sums[v] + term
+        value = jnp.zeros((8, LANES), jnp.float32)
+        for v in range(5):
+            value = jnp.where(row == v, jnp.sum(sums[v], axis=0, keepdims=True), value)
         first = tile * (LANES // width)
-        for v in range(5):
-            picked = lane_take(points[v], index)
-            donor_ref[first, v : v + 1, :] = jnp.sum(picked * scale, axis=0, keepdims=True)
+        donor_ref[first] = value
         for k in range(1, LANES // width):
-            donor_ref[first + k, :, :] = pltpu.roll(donor_ref[first], LANES - k * width, axis=1)
-
-
-def face_slots(points, plus_ref, minus_ref, face_matrix, slot_ref):
+            donor_ref[first + k] = pltpu.roll(value, LANES - k * width, axis=1)
+
+
+def face_slots(points, plus_ref, minus_ref, face_ref, factor, slot_ref):
+    centre = (1.0, 0.0, 0.0, 0.0, 2.5)
     for v in range(5):
-        centre = (1.0, 0.0, 0.0, 0.0, 2.5)[v]
-        faces = matmul(face_matrix, points[v] - centre) + centre
+        store_parts(factor, 0, v, points[v] - centre[v])
+    for v, faces in products(face_ref, factor):
         for side, order in ((0, plus_ref), (1, minus_ref)):
             for d in range(3):
                 start = (side * 3 + d) * ROWS
-                slot_ref[side, d, v] = lane_take(
+                slot_ref[side, d, v] = centre[v] + lane_take(
                     faces[start : start + ROWS], spread(order[d : d + 1, :], ROWS)
                 )
 
 
 def face_messages(slot_ref, message_ref):
-    count = message_ref.shape[0]
+    count = message_ref.shape[0] // 8
     for row in range(8):
         columns = [
             slot_ref[n // 15, n // 5 % 3, n % 5] for n in range(4 * row, min(4 * row + 4, 30))
         ]
         columns += [columns[-1]] * (4 - len(columns))
-        message_ref[:, row, :] = jnp.concatenate(columns, axis=0).T[0:count]
+        message_ref[pl.ds(row, count, stride=8), :] = jnp.concatenate(columns, axis=0).T[0:count]
+
+
+def partner_faces(partner_in, partner):
+    count = partner_in.shape[0] // 8
+    for row in range(8):
+        block = partner_in[pl.ds(row, count, stride=8), :]
+        block = jnp.concatenate([block] * (LANES // count), axis=0).T
+        partner[row * LANES : (row + 1) * LANES, :] = block
 
 
 def volume_terms(points, scale_ref, volume_ref, flux, total):
@@ -192,9 +232,9 @@
     for d in range(3):
         pieces = euler(w, d)[0]
         for v in range(5):
-            flux[v, d * LANES : (d + 1) * LANES, :] = pieces[v] * spread(scale_ref[d : d + 1, :], LANES)
-    for v in range(5):
-        total[v] = matmul(volume_ref[...], flux[v])
+            store_parts(flux, d * LANES, v, pieces[v] * spread(scale_ref[d : d + 1, :], LANES))
+    for v, value in products(volume_ref, flux):
+        total[v] = value
 
 
 def inverse_orders(plus_ref, minus_ref, inverse):
@@ -260,7 +300,7 @@
                 jump[v, start : start + ROWS, :] = lane_take(value[v], back) * scale
 
 
-def fringe_jumps(remote, arrived_ref, pick, own, by_grid, scale_ref, inverse, jump):
+def fringe_jumps(remote, arrived_ref, pick, own, by_grid, scale_ref, inverse, jump, factor):
     parts, slots, width = arrived_ref.shape
     grids = by_grid.shape[0]
     each = parts * slots
@@ -269,13 +309,11 @@
     by_grid[...] = turned[0 : grids * 8].reshape(grids, 8, LANES)
     chosen = pick[...]
     owner, place = chosen // each, chosen - each * (chosen // each)
-    outside = []
-    for v in range(5):
-        value = lane_take(spread(by_grid[0, v : v + 1, :], 8), place)
-        for g in range(1, grids):
+    outside = [None] * 5
+    for g in range(grids):
+        for v in range(5):
             source = lane_take(spread(by_grid[g, v : v + 1, :], 8), place)
-            value = jnp.where(owner == g, source, value)
-        outside.append(value)
+            outside[v] = source if g == 0 else jnp.where(owner == g, source, outside[v])
     inside = [own[v] for v in range(5)]
     lane = lax.broadcasted_iota(jnp.int32, (8, LANES), 1)
     face = lane // 4 - 6 * (lane // 24)
@@ -289,16 +327,18 @@
         0.5 * (a + b) - wave * (o - i)
         for a, b, o, i in zip(outer_flux, inner_flux, outside, inside)
     ]
-    for k in range(6):
-        slot = inverse[k] - remote
-        here = (slot >= 0) & (slot < FRP)
-        slot = jnp.where(here, slot, 0) + 4 * k
-        scale = spread(scale_ref[k % 3 : k % 3 + 1, :], 8)
-        for block in range(4):
-            rows = slice(k * ROWS + 8 * block, k * ROWS + 8 * block + 8)
-            for v in range(5):
+    for v in range(5):
+        for k in range(6):
+            slot = inverse[k] - remote
+            here = (slot >= 0) & (slot < FRP)
+            slot = jnp.where(here, slot, 0) + 4 * k
+            scale = spread(scale_ref[k % 3 : k % 3 + 1, :], 8)
+            blocks = []
+            for block in range(4):
+                start = k * ROWS + 8 * block
                 new = lane_take(value[v], slot + 24 * block) * scale
-                jump[v, rows, :] = jnp.where(here, new, jump[v, rows, :])
+                blocks.append(jnp.where(here, new, jump[v, start : start + 8, :]))
+            store_parts(factor, k * ROWS, v, jnp.concatenate(blocks, axis=0))
 
 
 def ring_distance(offset, size):
@@ -311,17 +351,26 @@
     face_ref, volume_ref, lift_ref = buffers[7:]
     (
         points, pair_weight, weight, donor, slot, message, partner_in, gathered, relay, arrived,
-        flux, total, inverse, pick_rows, pick, own, partner, jump, by_grid,
+        face_factor, flux, lift_factor, total, inverse, pick_rows, pick, own, partner, jump, by_grid,
         load_sem, sends, recvs,
     ) = scratch
+    loads = [
+        pltpu.make_async_copy(source, target, load_sem.at[n])
+        for n, (source, target) in enumerate(zip(inputs, buffers))
+    ]
+    for n in (0, 4, 5):
+        loads[n].start()
     grid = lax.axis_index("grid")
     part = lax.axis_index("dom")
     across = 4 if parts % 4 == 0 else 1
     down = parts // across
-
-    def part_at(offset):
-        z, x = offset // across, offset % across
-        return lax.rem(part // across + z, down) * across + lax.rem(lax.rem(part, across) + x, across)
+    z, x = part // across, lax.rem(part, across)
+    along_z = [lax.rem(z + k, down) * across for k in range(down)]
+    along_x = [lax.rem(x + k, across) for k in range(across)]
+    along_grid = [lax.rem(grid + k, grids) for k in range(grids)]
+
+    def part_at(k):
+        return along_z[k // across] + along_x[k % across]
 
     grid_steps = sorted(range(1, grids), key=lambda k: -ring_distance(k, grids))
     part_steps = sorted(
@@ -332,53 +381,45 @@
     for k in part_steps:
         pl.semaphore_signal(barrier, inc=1, device_id=(grid, part_at(k)), device_id_type=MESH)
     for k in grid_steps:
-        pl.semaphore_signal(
-            barrier, inc=1, device_id=(lax.rem(grid + k, grids), part), device_id_type=MESH
-        )
-    loads = [
-        pltpu.make_async_copy(source, target, load_sem.at[n])
-        for n, (source, target) in enumerate(zip(inputs, buffers))
-    ]
-    for n in (0, 4, 5, 2, 3, 7, 1, 6, 8, 9):
+        pl.semaphore_signal(barrier, inc=1, device_id=(along_grid[k], part), device_id_type=MESH)
+    for n in (2, 3, 7, 1, 6, 8, 9):
         loads[n].start()
 
-    def to_grid(k):
-        peer = lax.rem(grid + k, grids)
-        return pltpu.make_async_remote_copy(
-            src_ref=donor.at[peer], dst_ref=gathered.at[grid],
-            send_sem=sends.at[k - 1], recv_sem=recvs.at[k - 1],
-            device_id=(peer, part), device_id_type=MESH,
-        )
-
-    def to_part(k, source, target, base):
-        peer = part_at(k)
-        return pltpu.make_async_remote_copy(
-            src_ref=source.at[peer], dst_ref=target.at[part],
-            send_sem=sends.at[base + k - 1], recv_sem=recvs.at[base + k - 1],
-            device_id=(grid, peer), device_id_type=MESH,
-        )
-
-    first = [to_grid(k) for k in grid_steps]
-    faces = [to_part(k, message, partner_in, grids - 1) for k in part_steps]
-    second = [to_part(k, relay, arrived, grids + parts - 2) for k in part_steps]
+    def stage(n, source, target, grid_steps=(), part_steps=(), tall=None):
+        copies = []
+        for k in grid_steps:
+            copies.append((along_grid[k], part, along_grid[k], grid))
+        for k in part_steps:
+            copies.append((grid, part_at(k), part_at(k), part))
+        for to_grid, to_part, place, mine in copies:
+            if tall is not None:
+                place, mine = (pl.ds(pl.multiple_of(p * tall, tall), tall) for p in (place, mine))
+            pltpu.make_async_remote_copy(
+                src_ref=source.at[place], dst_ref=target.at[mine],
+                send_sem=sends.at[n], recv_sem=recvs.at[n],
+                device_id=(to_grid, to_part), device_id_type=MESH,
+            ).start()
+
+    def finish(semaphore, buffer, count):
+        whole = buffer.at[pl.ds(0, count)]
+        pltpu.make_async_copy(whole, whole, semaphore).wait()
 
     loads[0].wait()
     load_state(state_ref, points)
     loads[4].wait()
     loads[5].wait()
     donor_values(points, cell_ref, weight_ref, pair_weight, weight, donor)
+    pl.semaphore_wait(barrier, grids + parts - 2)
+    stage(0, donor, gathered, grid_steps=grid_steps)
+    gathered[grid] = donor[grid]
+
     for n in (2, 3, 7):
         loads[n].wait()
-    face_slots(points, plus_ref, minus_ref, face_ref[...], slot)
+    face_slots(points, plus_ref, minus_ref, face_ref, face_factor, slot)
     face_messages(slot, message)
-
-    pl.semaphore_wait(barrier, grids + parts - 2)
-    for copy in first:
-        copy.start()
-    for copy in faces:
-        copy.start()
-    gathered[grid] = donor[grid]
-    partner_in[part] = message[part]
+    stage(1, message, partner_in, part_steps=part_steps, tall=8)
+    mine = pl.ds(pl.multiple_of(part * 8, 8), 8)
+    partner_in[mine, :] = message[mine, :]
 
     for n in (1, 6, 8, 9):
         loads[n].wait()
@@ -387,32 +428,25 @@
     fringe_picks(pick_ref, pick_rows, pick)
     fringe_own(slot, parts, own)
 
-    for copy in first:
-        copy.wait_recv()
+    finish(recvs.at[0], gathered, grids - 1)
     turned = gathered[...].reshape(grids * 8, LANES)
     if grids * 8 < LANES:
         turned = jnp.concatenate([turned] * (LANES // (grids * 8)), axis=0)
     relay[...] = turned.T[0 : relay.shape[0] * relay.shape[1]].reshape(relay.shape)
-    for copy in second:
-        copy.start()
+    stage(2, relay, arrived, part_steps=part_steps)
     arrived[part] = relay[part]
 
-    for copy in faces:
-        copy.wait_recv()
-    for row in range(8):
-        block = partner_in[:, row, :]
-        block = jnp.concatenate([block] * (LANES // parts), axis=0).T
-        partner[row * LANES : (row + 1) * LANES, :] = block
+    finish(recvs.at[1], partner_in, 8 * (parts - 1))
+    partner_faces(partner_in, partner)
     inner_jumps(parts, slot, partner, scale_ref, inverse, jump)
-
-    for copy in second:
-        copy.wait_recv()
-    fringe_jumps(parts, arrived, pick, own, by_grid, scale_ref, inverse, jump)
-    for v in range(5):
-        value = total[v] + matmul(lift_ref[...], jump[v])
-        out_ref[v] = value[0:125]
-    for copy in first + faces + second:
-        copy.wait_send()
+    finish(sends.at[0], donor, grids - 1)
+    finish(sends.at[1], message, 8 * (parts - 1))
+    finish(sends.at[2], relay, parts - 1)
+
+    finish(recvs.at[2], arrived, parts - 1)
+    fringe_jumps(parts, arrived, pick, own, by_grid, scale_ref, inverse, jump, lift_factor)
+    for v, value in products(lift_ref, lift_factor):
+        out_ref[v] = (total[v] + value)[0:125]
 
 
 def body(grids, parts, state, scales, plus, minus, cell, weights, picks):
@@ -421,12 +455,11 @@
     slots = total_slots // (grids * parts)
     weights = jnp.transpose(weights, (1, 2, 0, 3))
     inputs = (state, scales, plus, minus, cell, weights, picks) + matrices()
-    copies = grids - 1 + 2 * (parts - 1)
     pick_tiles = -(-picks.shape[-1] // LANES)
     return pl.pallas_call(
         functools.partial(kernel, grids, parts),
         out_shape=jax.ShapeDtypeStruct(state.shape, f32),
-        in_specs=[pl.BlockSpec(memory_space=pl.ANY)] * len(inputs),
+        in_specs=[pl.BlockSpec(memory_space=pltpu.HBM)] * len(inputs),
         out_specs=pl.BlockSpec(memory_space=pltpu.VMEM),
         scratch_shapes=[pltpu.VMEM(x.shape, x.dtype) for x in inputs]
         + [
@@ -435,12 +468,14 @@
             pltpu.VMEM((LANES, total_slots), f32),
             pltpu.VMEM((grids, 8, LANES), f32),
             pltpu.VMEM((2, 3, 5, ROWS, LANES), f32),
-            pltpu.VMEM((parts, 8, LANES), f32),
-            pltpu.VMEM((parts, 8, LANES), f32),
+            pltpu.VMEM((parts * 8, LANES), f32),
+            pltpu.VMEM((parts * 8, LANES), f32),
             pltpu.VMEM((grids, 8, LANES), f32),
             pltpu.VMEM((parts, slots, LANES), f32),
             pltpu.VMEM((parts, slots, LANES), f32),
-            pltpu.VMEM((5, 3 * LANES, LANES), f32),
+            pltpu.VMEM((3 * LANES, 5 * LANES), jnp.bfloat16),
+            pltpu.VMEM((9 * LANES, 5 * LANES), jnp.bfloat16),
+            pltpu.VMEM((18 * ROWS, 5 * LANES), jnp.bfloat16),
             pltpu.VMEM((5, LANES, LANES), f32),
             pltpu.VMEM((6, 8, LANES), i32),
             pltpu.VMEM((8, pick_tiles * LANES), i32),
@@ -450,12 +485,14 @@
             pltpu.VMEM((5, 6 * ROWS, LANES), f32),
             pltpu.VMEM((grids, 8, LANES), f32),
             pltpu.SemaphoreType.DMA((len(inputs),)),
-            pltpu.SemaphoreType.DMA((copies,)),
-            pltpu.SemaphoreType.DMA((copies,)),
+            pltpu.SemaphoreType.DMA((3,)),
+            pltpu.SemaphoreType.DMA((3,)),
         ],
-        compiler_params=pltpu.CompilerParams(collective_id=0, has_side_effects=True),
+        compiler_params=pltpu.CompilerParams(
+            collective_id=0, has_side_effects=True, vmem_limit_bytes=24 * 1024 * 1024
+        ),
         name="step",
-    )(*inputs)
+    )(*(pltpu.with_memory_space_constraint(x, pltpu.HBM) for x in inputs))
 
 
 def solution(mesh):

time: 31.2 us -> 28 us (0.90)
  Pallas kernels: 29.3 us -> 27.1 us
  local copies, waits for them, and re-layouts: 1.72 us -> 0.73 us
    pallas_call x1, Pallas kernels: 29.3 us -> 27.1 us  [body(): pl.pallas_call(functools.partial(kernel, grids, parts), out_shape=jax.Sha...]
    unnamed x1, local copies, waits for them, and re-layouts: 1.72 us -> 0.73 us
where the time goes in v3:
time: 28 us; the launch traced here: 27.9 us
  Pallas kernels  27.1 us (97%)
  local copies, waits for them, and re-layouts  0.73 us (3%)
    pallas_call x1, Pallas kernels, body(): pl.pallas_call(functools.partial(kernel, grids, parts), out_shape=jax.Sha...  27.1 us
    unnamed x1, local copies, waits for them, and re-layouts  0.73 us

profile of v3, /device:TPU:1, one launch (start us, length us, event | category | flops | bytes accessed | tf_op | source)
XLA Modules:
  0.0 27.9 jit_solution(4002371104512401324)
XLA Ops:
  0.0 27.1 %step.1 = f32[5,125,128]{2,1,0:T(8,128)S(1)} custom-call(f32[5,125,128]{2,1,0:T(8,128)} %refs_0_.1, f32[3,128]{1,0:T(4,128)} %refs_1_.1, s32[3,128]{1,0:T(4,128)} %refs_2_.1, s32[3,128]{1,0:T(4,128)} %refs_3_.1, s32[1,1024]{1,0:T(1,128)} %refs_4_.1, f32[3,5,1,1024]{3,2,1,0:T(1,128)} %bitcast.1, s32[1,600]{1,0:T(1,128)} %refs_6_.1, ...), custom_call_target="tpu_custom_call" | custom-call | tf_op jit(solution)/shard_map/step/pallas_call | solution.py:459
  27.2 0.7 %copy.12 = f32[5,125,128]{2,1,0:T(8,128)} copy(f32[5,125,128]{2,1,0:T(8,128)S(1)} %step.1) | data formatting | bytes 640000

commit v4 on v3

--- a/solution.py
+++ b/solution.py
@@ -166,34 +166,31 @@
         points[v, 125:128, :] = state_ref[v, 122:125, :]
 
 
-def donor_values(points, cell_ref, weight_ref, pair_weight, weight, donor_ref):
-    slots = cell_ref.shape[-1]
-    grids = donor_ref.shape[0]
-    width = slots // grids
-    weight[120:128, :] = jnp.zeros((8, slots), jnp.float32)
+def donor_tile(tile, points, cell_ref, weight_ref, pair_weight, weight, donor_ref):
+    per_tile = LANES * donor_ref.shape[0] // cell_ref.shape[-1]
+    lanes = pl.ds(pl.multiple_of(tile * LANES, LANES), LANES)
+    scales = [[weight_ref[d, k, :, lanes] for k in range(5)] for d in range(3)]
     for b in range(5):
         for c in range(5):
             row = 5 * b + c
-            pair_weight[row : row + 1, :] = weight_ref[1, b] * weight_ref[2, c]
+            pair_weight[row : row + 1, :] = scales[1][b] * scales[2][c]
+    weight[120:128, :] = jnp.zeros((8, LANES), jnp.float32)
     for a in range(5):
-        weight[25 * a : 25 * a + 25, :] = weight_ref[0, a] * pair_weight[0:25, :]
+        weight[25 * a : 25 * a + 25, :] = scales[0][a] * pair_weight[0:25, :]
+    index = spread(cell_ref[0:1, lanes], 8)
+    sums = [None] * 5
+    for k in range(LANES // 8):
+        scale = weight[8 * k : 8 * k + 8, :]
+        for v in range(5):
+            term = lane_take(points[v, 8 * k : 8 * k + 8, :], index) * scale
+            sums[v] = term if k == 0 else sums[v] + term
     row = lax.broadcasted_iota(jnp.int32, (8, LANES), 0)
-    for tile in range(slots // LANES):
-        lanes = slice(tile * LANES, (tile + 1) * LANES)
-        index = spread(cell_ref[0:1, lanes], 8)
-        sums = [None] * 5
-        for k in range(LANES // 8):
-            scale = weight[8 * k : 8 * k + 8, lanes]
-            for v in range(5):
-                term = lane_take(points[v, 8 * k : 8 * k + 8, :], index) * scale
-                sums[v] = term if k == 0 else sums[v] + term
-        value = jnp.zeros((8, LANES), jnp.float32)
-        for v in range(5):
-            value = jnp.where(row == v, jnp.sum(sums[v], axis=0, keepdims=True), value)
-        first = tile * (LANES // width)
-        donor_ref[first] = value
-        for k in range(1, LANES // width):
-            donor_ref[first + k] = pltpu.roll(value, LANES - k * width, axis=1)
+    value = jnp.zeros((8, LANES), jnp.float32)
+    for v in range(5):
+        value = jnp.where(row == v, jnp.sum(sums[v], axis=0, keepdims=True), value)
+    donor_ref[tile * per_tile] = value
+    for k in range(1, per_tile):
+        donor_ref[tile * per_tile + k] = pltpu.roll(value, LANES - k * (LANES // per_tile), axis=1)
 
 
 def face_slots(points, plus_ref, minus_ref, face_ref, factor, slot_ref):
@@ -385,20 +382,12 @@
     for n in (2, 3, 7, 1, 6, 8, 9):
         loads[n].start()
 
-    def stage(n, source, target, grid_steps=(), part_steps=(), tall=None):
-        copies = []
-        for k in grid_steps:
-            copies.append((along_grid[k], part, along_grid[k], grid))
-        for k in part_steps:
-            copies.append((grid, part_at(k), part_at(k), part))
-        for to_grid, to_part, place, mine in copies:
-            if tall is not None:
-                place, mine = (pl.ds(pl.multiple_of(p * tall, tall), tall) for p in (place, mine))
-            pltpu.make_async_remote_copy(
-                src_ref=source.at[place], dst_ref=target.at[mine],
-                send_sem=sends.at[n], recv_sem=recvs.at[n],
-                device_id=(to_grid, to_part), device_id_type=MESH,
-            ).start()
+    def send(n, source, place, target, mine, to_grid, to_part):
+        pltpu.make_async_remote_copy(
+            src_ref=source.at[place], dst_ref=target.at[mine],
+            send_sem=sends.at[n], recv_sem=recvs.at[n],
+            device_id=(to_grid, to_part), device_id_type=MESH,
+        ).start()
 
     def finish(semaphore, buffer, count):
         whole = buffer.at[pl.ds(0, count)]
@@ -408,17 +397,30 @@
     load_state(state_ref, points)
     loads[4].wait()
     loads[5].wait()
-    donor_values(points, cell_ref, weight_ref, pair_weight, weight, donor)
-    pl.semaphore_wait(barrier, grids + parts - 2)
-    stage(0, donor, gathered, grid_steps=grid_steps)
+    tiles = cell_ref.shape[-1] // LANES
+    per_tile = grids // tiles
+    near = grid // per_tile
+    for n, step in enumerate(sorted(range(tiles), key=lambda k: -ring_distance(k, tiles))):
+        tile = lax.rem(near + step, tiles)
+        donor_tile(
+            tile, points, cell_ref, weight_ref, pair_weight.at[n % 2], weight.at[n % 2], donor
+        )
+        if n == 0:
+            pl.semaphore_wait(barrier, grids + parts - 2)
+        for k in range(per_tile if step else per_tile - 1):
+            first = lax.rem(grid, per_tile) + 1 if step == 0 else 0
+            peer = tile * per_tile + lax.rem(first + k, per_tile)
+            send(0, donor, peer, gathered, grid, peer, part)
     gathered[grid] = donor[grid]
 
     for n in (2, 3, 7):
         loads[n].wait()
     face_slots(points, plus_ref, minus_ref, face_ref, face_factor, slot)
     face_messages(slot, message)
-    stage(1, message, partner_in, part_steps=part_steps, tall=8)
     mine = pl.ds(pl.multiple_of(part * 8, 8), 8)
+    for k in part_steps:
+        peer = part_at(k)
+        send(1, message, pl.ds(pl.multiple_of(peer * 8, 8), 8), partner_in, mine, grid, peer)
     partner_in[mine, :] = message[mine, :]
 
     for n in (1, 6, 8, 9):
@@ -433,7 +435,9 @@
     if grids * 8 < LANES:
         turned = jnp.concatenate([turned] * (LANES // (grids * 8)), axis=0)
     relay[...] = turned.T[0 : relay.shape[0] * relay.shape[1]].reshape(relay.shape)
-    stage(2, relay, arrived, part_steps=part_steps)
+    for k in part_steps:
+        peer = part_at(k)
+        send(2, relay, peer, arrived, part, grid, peer)
     arrived[part] = relay[part]
 
     finish(recvs.at[1], partner_in, 8 * (parts - 1))
@@ -464,8 +468,8 @@
         scratch_shapes=[pltpu.VMEM(x.shape, x.dtype) for x in inputs]
         + [
             pltpu.VMEM((5, LANES, LANES), f32),
-            pltpu.VMEM((32, total_slots), f32),
-            pltpu.VMEM((LANES, total_slots), f32),
+            pltpu.VMEM((2, 32, LANES), f32),
+            pltpu.VMEM((2, LANES, LANES), f32),
             pltpu.VMEM((grids, 8, LANES), f32),
             pltpu.VMEM((2, 3, 5, ROWS, LANES), f32),
             pltpu.VMEM((parts * 8, LANES), f32),

time: 28 us -> 27.9 us (level)
  no operation moved by 1% of the time
where the time goes in v4:
time: 27.9 us; the launch traced here: 27.8 us
  Pallas kernels  27.1 us (97%)
  local copies, waits for them, and re-layouts  0.73 us (3%)
    pallas_call x1, Pallas kernels, body(): pl.pallas_call(functools.partial(kernel, grids, parts), out_shape=jax.Sha...  27.1 us
    unnamed x1, local copies, waits for them, and re-layouts  0.73 us

profile of v4, /device:TPU:1, one launch (start us, length us, event | category | flops | bytes accessed | tf_op | source)
XLA Modules:
  0.0 27.8 jit_solution(10342344095187294179)
XLA Ops:
  0.0 27.1 %step.1 = f32[5,125,128]{2,1,0:T(8,128)S(1)} custom-call(f32[5,125,128]{2,1,0:T(8,128)} %refs_0_.1, f32[3,128]{1,0:T(4,128)} %refs_1_.1, s32[3,128]{1,0:T(4,128)} %refs_2_.1, s32[3,128]{1,0:T(4,128)} %refs_3_.1, s32[1,1024]{1,0:T(1,128)} %refs_4_.1, f32[3,5,1,1024]{3,2,1,0:T(1,128)} %bitcast.1, s32[1,600]{1,0:T(1,128)} %refs_6_.1, ...), custom_call_target="tpu_custom_call" | custom-call | tf_op jit(solution)/shard_map/step/pallas_call | solution.py:463
  27.1 0.7 %copy.12 = f32[5,125,128]{2,1,0:T(8,128)} copy(f32[5,125,128]{2,1,0:T(8,128)S(1)} %step.1) | data formatting | bytes 640000

commit v5 on v4

--- a/solution.py
+++ b/solution.py
@@ -168,7 +168,7 @@
 
 def donor_tile(tile, points, cell_ref, weight_ref, pair_weight, weight, donor_ref):
     per_tile = LANES * donor_ref.shape[0] // cell_ref.shape[-1]
-    lanes = pl.ds(pl.multiple_of(tile * LANES, LANES), LANES)
+    lanes = slice(tile * LANES, (tile + 1) * LANES)
     scales = [[weight_ref[d, k, :, lanes] for k in range(5)] for d in range(3)]
     for b in range(5):
         for c in range(5):
@@ -297,13 +297,8 @@
                 jump[v, start : start + ROWS, :] = lane_take(value[v], back) * scale
 
 
-def fringe_jumps(remote, arrived_ref, pick, own, by_grid, scale_ref, inverse, jump, factor):
-    parts, slots, width = arrived_ref.shape
+def fringe_jumps(remote, each, pick, own, by_grid, scale_ref, inverse, jump, factor):
     grids = by_grid.shape[0]
-    each = parts * slots
-    turned = arrived_ref[...].reshape(each, width)
-    turned = jnp.concatenate([turned] * (LANES // each), axis=0).T
-    by_grid[...] = turned[0 : grids * 8].reshape(grids, 8, LANES)
     chosen = pick[...]
     owner, place = chosen // each, chosen - each * (chosen // each)
     outside = [None] * 5
@@ -347,9 +342,9 @@
     (state_ref, scale_ref, plus_ref, minus_ref, cell_ref, weight_ref, pick_ref) = buffers[:7]
     face_ref, volume_ref, lift_ref = buffers[7:]
     (
-        points, pair_weight, weight, donor, slot, message, partner_in, gathered, relay, arrived,
+        points, pair_weight, weight, donor, slot, message, partner_in, outgoing, incoming, relay,
         face_factor, flux, lift_factor, total, inverse, pick_rows, pick, own, partner, jump, by_grid,
-        load_sem, sends, recvs,
+        load_sem, sends, recvs, entered,
     ) = scratch
     loads = [
         pltpu.make_async_copy(source, target, load_sem.at[n])
@@ -364,21 +359,30 @@
     z, x = part // across, lax.rem(part, across)
     along_z = [lax.rem(z + k, down) * across for k in range(down)]
     along_x = [lax.rem(x + k, across) for k in range(across)]
-    along_grid = [lax.rem(grid + k, grids) for k in range(grids)]
+    chips = grids // 2
+    assert chips in (1, 2, 4, 8)
+    core = lax.rem(grid, 2)
+    along_y = [lax.rem(grid // 2 + k, chips) * 2 for k in range(chips)]
 
     def part_at(k):
         return along_z[k // across] + along_x[k % across]
 
-    grid_steps = sorted(range(1, grids), key=lambda k: -ring_distance(k, grids))
+    def cores_at(k):
+        other = along_y[k] + 1 - core
+        return [along_y[k] + core, other] if k else [other]
+
+    chip_steps = sorted(range(chips), key=lambda k: -ring_distance(k, chips))
     part_steps = sorted(
         range(1, parts),
         key=lambda k: -(ring_distance(k // across, down) + ring_distance(k % across, across)),
     )
+    near = [peer for k in chip_steps if ring_distance(k, chips) <= 2 for peer in cores_at(k)]
+    relays = sorted({2 % chips, -2 % chips} - {0})
     barrier = pltpu.get_barrier_semaphore()
     for k in part_steps:
         pl.semaphore_signal(barrier, inc=1, device_id=(grid, part_at(k)), device_id_type=MESH)
-    for k in grid_steps:
-        pl.semaphore_signal(barrier, inc=1, device_id=(along_grid[k], part), device_id_type=MESH)
+    for peer in near:
+        pl.semaphore_signal(barrier, inc=1, device_id=(peer, part), device_id_type=MESH)
     for n in (2, 3, 7, 1, 6, 8, 9):
         loads[n].start()
 
@@ -397,21 +401,23 @@
     load_state(state_ref, points)
     loads[4].wait()
     loads[5].wait()
-    tiles = cell_ref.shape[-1] // LANES
-    per_tile = grids // tiles
-    near = grid // per_tile
-    for n, step in enumerate(sorted(range(tiles), key=lambda k: -ring_distance(k, tiles))):
-        tile = lax.rem(near + step, tiles)
+    for tile in range(cell_ref.shape[-1] // LANES):
         donor_tile(
-            tile, points, cell_ref, weight_ref, pair_weight.at[n % 2], weight.at[n % 2], donor
+            tile, points, cell_ref, weight_ref, pair_weight.at[tile % 2], weight.at[tile % 2], donor
         )
-        if n == 0:
-            pl.semaphore_wait(barrier, grids + parts - 2)
-        for k in range(per_tile if step else per_tile - 1):
-            first = lax.rem(grid, per_tile) + 1 if step == 0 else 0
-            peer = tile * per_tile + lax.rem(first + k, per_tile)
-            send(0, donor, peer, gathered, grid, peer, part)
-    gathered[grid] = donor[grid]
+    turned = donor[...].reshape(grids * 8, LANES)
+    turned = jnp.concatenate([turned] * (LANES // (grids * 8)), axis=0).T
+    each = outgoing.shape[0] * outgoing.shape[1]
+    outgoing[...] = turned[0:each].reshape(outgoing.shape)
+    pl.semaphore_wait(barrier, parts - 1 + len(near))
+    for k in part_steps:
+        peer = part_at(k)
+        send(0, outgoing, peer, incoming, part, grid, peer)
+    for k in relays:
+        pl.semaphore_signal(
+            entered, inc=1, device_id=(along_y[k] + core, part), device_id_type=MESH
+        )
+    incoming[part] = outgoing[part]
 
     for n in (2, 3, 7):
         loads[n].wait()
@@ -430,25 +436,26 @@
     fringe_picks(pick_ref, pick_rows, pick)
     fringe_own(slot, parts, own)
 
-    finish(recvs.at[0], gathered, grids - 1)
-    turned = gathered[...].reshape(grids * 8, LANES)
-    if grids * 8 < LANES:
-        turned = jnp.concatenate([turned] * (LANES // (grids * 8)), axis=0)
-    relay[...] = turned.T[0 : relay.shape[0] * relay.shape[1]].reshape(relay.shape)
-    for k in part_steps:
-        peer = part_at(k)
-        send(2, relay, peer, arrived, part, grid, peer)
-    arrived[part] = relay[part]
+    finish(recvs.at[0], incoming, parts - 1)
+    turned = incoming[...].reshape(each, LANES)
+    turned = jnp.concatenate([turned] * (LANES // each), axis=0).T
+    relay[...] = turned[0 : grids * 8].reshape(relay.shape)
+    if relays:
+        pl.semaphore_wait(entered, len(relays))
+    for k in chip_steps:
+        for peer in cores_at(k):
+            send(2, relay, peer, by_grid, grid, peer, part)
+    by_grid[grid] = relay[grid]
 
     finish(recvs.at[1], partner_in, 8 * (parts - 1))
     partner_faces(partner_in, partner)
     inner_jumps(parts, slot, partner, scale_ref, inverse, jump)
-    finish(sends.at[0], donor, grids - 1)
+    finish(sends.at[0], outgoing, parts - 1)
     finish(sends.at[1], message, 8 * (parts - 1))
-    finish(sends.at[2], relay, parts - 1)
-
-    finish(recvs.at[2], arrived, parts - 1)
-    fringe_jumps(parts, arrived, pick, own, by_grid, scale_ref, inverse, jump, lift_factor)
+    finish(sends.at[2], relay, grids - 1)
+
+    finish(recvs.at[2], by_grid, grids - 1)
+    fringe_jumps(parts, each, pick, own, by_grid, scale_ref, inverse, jump, lift_factor)
     for v, value in products(lift_ref, lift_factor):
         out_ref[v] = (total[v] + value)[0:125]
 
@@ -474,9 +481,9 @@
             pltpu.VMEM((2, 3, 5, ROWS, LANES), f32),
             pltpu.VMEM((parts * 8, LANES), f32),
             pltpu.VMEM((parts * 8, LANES), f32),
-            pltpu.VMEM((grids, 8, LANES), f32),
             pltpu.VMEM((parts, slots, LANES), f32),
             pltpu.VMEM((parts, slots, LANES), f32),
+            pltpu.VMEM((grids, 8, LANES), f32),
             pltpu.VMEM((3 * LANES, 5 * LANES), jnp.bfloat16),
             pltpu.VMEM((9 * LANES, 5 * LANES), jnp.bfloat16),
             pltpu.VMEM((18 * ROWS, 5 * LANES), jnp.bfloat16),
@@ -491,6 +498,7 @@
             pltpu.SemaphoreType.DMA((len(inputs),)),
             pltpu.SemaphoreType.DMA((3,)),
             pltpu.SemaphoreType.DMA((3,)),
+            pltpu.SemaphoreType.REGULAR,
         ],
         compiler_params=pltpu.CompilerParams(
             collective_id=0, has_side_effects=True, vmem_limit_bytes=24 * 1024 * 1024

time: 27.9 us -> 28.8 us (1.032)
  Pallas kernels: 27.1 us -> 27.9 us
    pallas_call x1, Pallas kernels: 27.1 us -> 27.9 us  [body(): pl.pallas_call(functools.partial(kernel, grids, parts), out_shape=jax.Sha...]
where the time goes in v5:
time: 28.8 us; the launch traced here: 28.6 us
  Pallas kernels  27.9 us (97%)
  local copies, waits for them, and re-layouts  0.73 us (3%)
    pallas_call x1, Pallas kernels, body(): pl.pallas_call(functools.partial(kernel, grids, parts), out_shape=jax.Sha...  27.9 us
    unnamed x1, local copies, waits for them, and re-layouts  0.73 us

profile of v5, /device:TPU:1, one launch (start us, length us, event | category | flops | bytes accessed | tf_op | source)
XLA Modules:
  0.0 28.6 jit_solution(16746555790496554968)
XLA Ops:
  0.0 27.9 %step.1 = f32[5,125,128]{2,1,0:T(8,128)S(1)} custom-call(f32[5,125,128]{2,1,0:T(8,128)} %refs_0_.1, f32[3,128]{1,0:T(4,128)} %refs_1_.1, s32[3,128]{1,0:T(4,128)} %refs_2_.1, s32[3,128]{1,0:T(4,128)} %refs_3_.1, s32[1,1024]{1,0:T(1,128)} %refs_4_.1, f32[3,5,1,1024]{3,2,1,0:T(1,128)} %bitcast.1, s32[1,600]{1,0:T(1,128)} %refs_6_.1, ...), custom_call_target="tpu_custom_call" | custom-call | tf_op jit(solution)/shard_map/step/pallas_call | solution.py:470
  27.9 0.7 %copy.12 = f32[5,125,128]{2,1,0:T(8,128)} copy(f32[5,125,128]{2,1,0:T(8,128)S(1)} %step.1) | data formatting | bytes 640000

commit v6 on v4

--- a/solution.py
+++ b/solution.py
@@ -13,6 +13,7 @@
 LANES = 128
 ROWS = 32
 FRP = 4
+ACROSS = 4
 
 
 def gauss_nodes():
@@ -166,25 +167,39 @@
         points[v, 125:128, :] = state_ref[v, 122:125, :]
 
 
-def donor_tile(tile, points, cell_ref, weight_ref, pair_weight, weight, donor_ref):
+def row_choice(row, values, index):
+    value = values[index[-1]]
+    for s in range(len(index) - 2, -1, -1):
+        if index[s] != index[s + 1]:
+            value = jnp.where(row <= s, values[index[s]], value)
+    return value
+
+
+def donor_tile(tile, points, cell_ref, weight_ref, donor_ref):
     per_tile = LANES * donor_ref.shape[0] // cell_ref.shape[-1]
     lanes = pl.ds(pl.multiple_of(tile * LANES, LANES), LANES)
-    scales = [[weight_ref[d, k, :, lanes] for k in range(5)] for d in range(3)]
-    for b in range(5):
-        for c in range(5):
-            row = 5 * b + c
-            pair_weight[row : row + 1, :] = scales[1][b] * scales[2][c]
-    weight[120:128, :] = jnp.zeros((8, LANES), jnp.float32)
-    for a in range(5):
-        weight[25 * a : 25 * a + 25, :] = scales[0][a] * pair_weight[0:25, :]
+    row = lax.broadcasted_iota(jnp.int32, (8, LANES), 0)
+    turn = row - 5 * (row // 5)
+    along = [[spread(weight_ref[d, k, :, lanes], 8) for k in range(5)] for d in range(3)]
+    last = []
+    for start in range(5):
+        value = along[2][(start + 4) % 5]
+        for k in range(4):
+            value = jnp.where(turn == k, along[2][(start + k) % 5], value)
+        last.append(value)
     index = spread(cell_ref[0:1, lanes], 8)
     sums = [None] * 5
     for k in range(LANES // 8):
-        scale = weight[8 * k : 8 * k + 8, :]
+        number = [min(8 * k + s, 124) for s in range(8)]
+        scale = row_choice(row, along[0], [p // 25 for p in number])
+        pairs = [p // 5 for p in number]
+        middle = row_choice(row, [along[1][p % 5] for p in range(25)], pairs)
+        scale = scale * middle * last[8 * k % 5]
+        if 8 * k + 8 > 125:
+            scale = jnp.where(row < 125 - 8 * k, scale, 0.0)
         for v in range(5):
             term = lane_take(points[v, 8 * k : 8 * k + 8, :], index) * scale
             sums[v] = term if k == 0 else sums[v] + term
-    row = lax.broadcasted_iota(jnp.int32, (8, LANES), 0)
     value = jnp.zeros((8, LANES), jnp.float32)
     for v in range(5):
         value = jnp.where(row == v, jnp.sum(sums[v], axis=0, keepdims=True), value)
@@ -347,9 +362,9 @@
     (state_ref, scale_ref, plus_ref, minus_ref, cell_ref, weight_ref, pick_ref) = buffers[:7]
     face_ref, volume_ref, lift_ref = buffers[7:]
     (
-        points, pair_weight, weight, donor, slot, message, partner_in, gathered, relay, arrived,
+        points, donor, slot, message, partner_in, gathered, relay, arrived,
         face_factor, flux, lift_factor, total, inverse, pick_rows, pick, own, partner, jump, by_grid,
-        load_sem, sends, recvs,
+        load_sem, sends, recvs, entered,
     ) = scratch
     loads = [
         pltpu.make_async_copy(source, target, load_sem.at[n])
@@ -359,26 +374,37 @@
         loads[n].start()
     grid = lax.axis_index("grid")
     part = lax.axis_index("dom")
-    across = 4 if parts % 4 == 0 else 1
-    down = parts // across
+    across, down = ACROSS, parts // ACROSS
+    half = down // 2
     z, x = part // across, lax.rem(part, across)
-    along_z = [lax.rem(z + k, down) * across for k in range(down)]
     along_x = [lax.rem(x + k, across) for k in range(across)]
     along_grid = [lax.rem(grid + k, grids) for k in range(grids)]
-
-    def part_at(k):
-        return along_z[k // across] + along_x[k % across]
-
-    grid_steps = sorted(range(1, grids), key=lambda k: -ring_distance(k, grids))
-    part_steps = sorted(
-        range(1, parts),
-        key=lambda k: -(ring_distance(k // across, down) + ring_distance(k % across, across)),
-    )
+    row_peers = [z * across + k for k in along_x[1:]]
+
+    def for_lower(act):
+        for k in range(down - 1, 0, -1):
+            @pl.when(z >= k)
+            def _(k=k):
+                for column in along_x:
+                    act((z - k) * across + column)
+
+    def for_higher(act, low, high):
+        for k in range(1, down):
+            @pl.when((z + k >= low) & (z + k < high))
+            def _(k=k):
+                for column in along_x:
+                    act((z + k) * across + column)
+
     barrier = pltpu.get_barrier_semaphore()
-    for k in part_steps:
-        pl.semaphore_signal(barrier, inc=1, device_id=(grid, part_at(k)), device_id_type=MESH)
-    for k in grid_steps:
+
+    def enter(peer):
+        pl.semaphore_signal(barrier, inc=1, device_id=(grid, peer), device_id_type=MESH)
+
+    for k in sorted(range(1, grids), key=lambda k: -ring_distance(k, grids)):
         pl.semaphore_signal(barrier, inc=1, device_id=(along_grid[k], part), device_id_type=MESH)
+    for peer in row_peers:
+        enter(peer)
+    for_higher(enter, 0, down)
     for n in (2, 3, 7, 1, 6, 8, 9):
         loads[n].start()
 
@@ -397,20 +423,24 @@
     load_state(state_ref, points)
     loads[4].wait()
     loads[5].wait()
+    def told(peer):
+        group = entered.at[z // max(half, 1)] if half else entered.at[0]
+        pl.semaphore_signal(group, inc=1, device_id=(grid, peer), device_id_type=MESH)
+
     tiles = cell_ref.shape[-1] // LANES
     per_tile = grids // tiles
     near = grid // per_tile
     for n, step in enumerate(sorted(range(tiles), key=lambda k: -ring_distance(k, tiles))):
         tile = lax.rem(near + step, tiles)
-        donor_tile(
-            tile, points, cell_ref, weight_ref, pair_weight.at[n % 2], weight.at[n % 2], donor
-        )
+        donor_tile(tile, points, cell_ref, weight_ref, donor)
         if n == 0:
-            pl.semaphore_wait(barrier, grids + parts - 2)
+            pl.semaphore_wait(barrier, grids - 1 + across * (z + 1) - 1)
         for k in range(per_tile if step else per_tile - 1):
             first = lax.rem(grid, per_tile) + 1 if step == 0 else 0
             peer = tile * per_tile + lax.rem(first + k, per_tile)
             send(0, donor, peer, gathered, grid, peer, part)
+        if n == 0:
+            for_lower(told)
     gathered[grid] = donor[grid]
 
     for n in (2, 3, 7):
@@ -418,9 +448,13 @@
     face_slots(points, plus_ref, minus_ref, face_ref, face_factor, slot)
     face_messages(slot, message)
     mine = pl.ds(pl.multiple_of(part * 8, 8), 8)
-    for k in part_steps:
-        peer = part_at(k)
+
+    def send_faces(peer):
         send(1, message, pl.ds(pl.multiple_of(peer * 8, 8), 8), partner_in, mine, grid, peer)
+
+    for_lower(send_faces)
+    for peer in row_peers:
+        send_faces(peer)
     partner_in[mine, :] = message[mine, :]
 
     for n in (1, 6, 8, 9):
@@ -435,10 +469,24 @@
     if grids * 8 < LANES:
         turned = jnp.concatenate([turned] * (LANES // (grids * 8)), axis=0)
     relay[...] = turned.T[0 : relay.shape[0] * relay.shape[1]].reshape(relay.shape)
-    for k in part_steps:
-        peer = part_at(k)
+    def send_donors(peer):
         send(2, relay, peer, arrived, part, grid, peer)
+
+    def send_both(peer):
+        send_donors(peer)
+        send_faces(peer)
+
+    for_lower(send_donors)
+    for peer in row_peers:
+        send_donors(peer)
     arrived[part] = relay[part]
+    for group, low, high in ((0, 0, half), (1, half, down)):
+        later = across * jnp.maximum(high - jnp.maximum(z + 1, low), 0)
+
+        @pl.when(later > 0)
+        def _():
+            pl.semaphore_wait(entered.at[group], later)
+            for_higher(send_both, low, high)
 
     finish(recvs.at[1], partner_in, 8 * (parts - 1))
     partner_faces(partner_in, partner)
@@ -468,8 +516,6 @@
         scratch_shapes=[pltpu.VMEM(x.shape, x.dtype) for x in inputs]
         + [
             pltpu.VMEM((5, LANES, LANES), f32),
-            pltpu.VMEM((2, 32, LANES), f32),
-            pltpu.VMEM((2, LANES, LANES), f32),
             pltpu.VMEM((grids, 8, LANES), f32),
             pltpu.VMEM((2, 3, 5, ROWS, LANES), f32),
             pltpu.VMEM((parts * 8, LANES), f32),
@@ -491,6 +537,7 @@
             pltpu.SemaphoreType.DMA((len(inputs),)),
             pltpu.SemaphoreType.DMA((3,)),
             pltpu.SemaphoreType.DMA((3,)),
+            pltpu.SemaphoreType.REGULAR((2,)),
         ],
         compiler_params=pltpu.CompilerParams(
             collective_id=0, has_side_effects=True, vmem_limit_bytes=24 * 1024 * 1024

time: 27.9 us -> 27.6 us (0.989)
  Pallas kernels: 27.1 us -> 26.7 us
    pallas_call x1, Pallas kernels: 27.1 us -> 26.7 us  [body(): pl.pallas_call(functools.partial(kernel, grids, parts), out_shape=jax.Sha...]
where the time goes in v6:
time: 27.6 us; the launch traced here: 27.5 us
  Pallas kernels  26.7 us (97%)
  local copies, waits for them, and re-layouts  0.73 us (3%)
    pallas_call x1, Pallas kernels, body(): pl.pallas_call(functools.partial(kernel, grids, parts), out_shape=jax.Sha...  26.7 us
    unnamed x1, local copies, waits for them, and re-layouts  0.73 us

profile of v6, /device:TPU:1, one launch (start us, length us, event | category | flops | bytes accessed | tf_op | source)
XLA Modules:
  0.0 27.5 jit_solution(12083893527617143323)
XLA Ops:
  0.0 26.7 %step.1 = f32[5,125,128]{2,1,0:T(8,128)S(1)} custom-call(f32[5,125,128]{2,1,0:T(8,128)} %refs_0_.1, f32[3,128]{1,0:T(4,128)} %refs_1_.1, s32[3,128]{1,0:T(4,128)} %refs_2_.1, s32[3,128]{1,0:T(4,128)} %refs_3_.1, s32[1,1024]{1,0:T(1,128)} %refs_4_.1, f32[3,5,1,1024]{3,2,1,0:T(1,128)} %bitcast.1, s32[1,600]{1,0:T(1,128)} %refs_6_.1, ...), custom_call_target="tpu_custom_call" | custom-call | tf_op jit(solution)/shard_map/step/pallas_call | solution.py:511
  26.7 0.7 %copy.12 = f32[5,125,128]{2,1,0:T(8,128)} copy(f32[5,125,128]{2,1,0:T(8,128)S(1)} %step.1) | data formatting | bytes 640000

commit v7 on v6

--- a/solution.py
+++ b/solution.py
@@ -367,11 +367,16 @@
         load_sem, sends, recvs, entered,
     ) = scratch
     loads = [
-        pltpu.make_async_copy(source, target, load_sem.at[n])
+        [
+            pltpu.make_async_copy(source.at[v], target.at[v], load_sem.at[len(inputs) + v])
+            for v in range(5)
+        ]
+        if n == 0
+        else pltpu.make_async_copy(source, target, load_sem.at[n])
         for n, (source, target) in enumerate(zip(inputs, buffers))
     ]
-    for n in (0, 4, 5):
-        loads[n].start()
+    for copy in loads[0] + loads[4:6]:
+        copy.start()
     grid = lax.axis_index("grid")
     part = lax.axis_index("dom")
     across, down = ACROSS, parts // ACROSS
@@ -419,50 +424,72 @@
         whole = buffer.at[pl.ds(0, count)]
         pltpu.make_async_copy(whole, whole, semaphore).wait()
 
-    loads[0].wait()
+    mine = pl.ds(pl.multiple_of(part * 8, 8), 8)
+
+    def told(peer):
+        group = entered.at[z // max(half, 1)] if half else entered.at[0]
+        pl.semaphore_signal(group, inc=1, device_id=(grid, peer), device_id_type=MESH)
+
+    def send_faces(peer):
+        send(1, message, pl.ds(pl.multiple_of(peer * 8, 8), 8), partner_in, mine, grid, peer)
+
+    tiles = cell_ref.shape[-1] // LANES
+    per_tile = grids // tiles
+    near = grid // per_tile
+    tile_steps = sorted(range(tiles), key=lambda k: -ring_distance(k, tiles))
+
+    def make_tile(step):
+        donor_tile(lax.rem(near + step, tiles), points, cell_ref, weight_ref, donor)
+
+    def send_tile(step):
+        first = lax.rem(grid, per_tile) + 1 if step == 0 else 0
+        for k in range(per_tile if step else per_tile - 1):
+            peer = lax.rem(near + step, tiles) * per_tile + lax.rem(first + k, per_tile)
+            send(0, donor, peer, gathered, grid, peer, part)
+
+    def make_faces():
+        for n in (2, 3, 7):
+            loads[n].wait()
+        face_slots(points, plus_ref, minus_ref, face_ref, face_factor, slot)
+        face_messages(slot, message)
+
+    def pass_barrier():
+        pl.semaphore_wait(barrier, grids - 1 + across * (z + 1) - 1)
+
+    for copy in loads[0]:
+        copy.wait()
     load_state(state_ref, points)
     loads[4].wait()
     loads[5].wait()
-    def told(peer):
-        group = entered.at[z // max(half, 1)] if half else entered.at[0]
-        pl.semaphore_signal(group, inc=1, device_id=(grid, peer), device_id_type=MESH)
-
-    tiles = cell_ref.shape[-1] // LANES
-    per_tile = grids // tiles
-    near = grid // per_tile
-    for n, step in enumerate(sorted(range(tiles), key=lambda k: -ring_distance(k, tiles))):
-        tile = lax.rem(near + step, tiles)
-        donor_tile(tile, points, cell_ref, weight_ref, donor)
-        if n == 0:
-            pl.semaphore_wait(barrier, grids - 1 + across * (z + 1) - 1)
-        for k in range(per_tile if step else per_tile - 1):
-            first = lax.rem(grid, per_tile) + 1 if step == 0 else 0
-            peer = tile * per_tile + lax.rem(first + k, per_tile)
-            send(0, donor, peer, gathered, grid, peer, part)
-        if n == 0:
-            for_lower(told)
-    gathered[grid] = donor[grid]
-
-    for n in (2, 3, 7):
-        loads[n].wait()
-    face_slots(points, plus_ref, minus_ref, face_ref, face_factor, slot)
-    face_messages(slot, message)
-    mine = pl.ds(pl.multiple_of(part * 8, 8), 8)
-
-    def send_faces(peer):
-        send(1, message, pl.ds(pl.multiple_of(peer * 8, 8), 8), partner_in, mine, grid, peer)
+
+    late = (near == tiles // 2) | (near == tiles // 2 + 1)
+
+    @pl.when(late)
+    def _():
+        for n, step in enumerate(tile_steps):
+            make_tile(step)
+            if n == 0:
+                pass_barrier()
+            send_tile(step)
+            if n == 0:
+                for_lower(told)
+        make_faces()
+
+    @pl.when(jnp.logical_not(late))
+    def _():
+        for step in tile_steps:
+            make_tile(step)
+        make_faces()
+        pass_barrier()
+        for step in tile_steps:
+            send_tile(step)
+        for_lower(told)
 
     for_lower(send_faces)
     for peer in row_peers:
         send_faces(peer)
+    gathered[grid] = donor[grid]
     partner_in[mine, :] = message[mine, :]
-
-    for n in (1, 6, 8, 9):
-        loads[n].wait()
-    volume_terms(points, scale_ref, volume_ref, flux, total)
-    inverse_orders(plus_ref, minus_ref, inverse)
-    fringe_picks(pick_ref, pick_rows, pick)
-    fringe_own(slot, parts, own)
 
     finish(recvs.at[0], gathered, grids - 1)
     turned = gathered[...].reshape(grids * 8, LANES)
@@ -480,6 +507,13 @@
     for peer in row_peers:
         send_donors(peer)
     arrived[part] = relay[part]
+
+    for n in (1, 6, 8, 9):
+        loads[n].wait()
+    volume_terms(points, scale_ref, volume_ref, flux, total)
+    inverse_orders(plus_ref, minus_ref, inverse)
+    fringe_picks(pick_ref, pick_rows, pick)
+    fringe_own(slot, parts, own)
     for group, low, high in ((0, 0, half), (1, half, down)):
         later = across * jnp.maximum(high - jnp.maximum(z + 1, low), 0)
 
@@ -534,7 +568,7 @@
             pltpu.VMEM((8 * LANES, LANES), f32),
             pltpu.VMEM((5, 6 * ROWS, LANES), f32),
             pltpu.VMEM((grids, 8, LANES), f32),
-            pltpu.SemaphoreType.DMA((len(inputs),)),
+            pltpu.SemaphoreType.DMA((len(inputs) + 5,)),
             pltpu.SemaphoreType.DMA((3,)),
             pltpu.SemaphoreType.DMA((3,)),
             pltpu.SemaphoreType.REGULAR((2,)),

time: 27.6 us -> 25.7 us (0.931)
  Pallas kernels: 26.7 us -> 24.8 us
    pallas_call x1, Pallas kernels: 26.7 us -> 24.8 us  [body(): pl.pallas_call(functools.partial(kernel, grids, parts), out_shape=jax.Sha...]
where the time goes in v7:
time: 25.7 us; the launch traced here: 25.5 us
  Pallas kernels  24.8 us (96%)
  local copies, waits for them, and re-layouts  0.73 us (3%)
    pallas_call x1, Pallas kernels, body(): pl.pallas_call(functools.partial(kernel, grids, parts), out_shape=jax.Sha...  24.8 us
    unnamed x1, local copies, waits for them, and re-layouts  0.73 us

profile of v7, /device:TPU:1, one launch (start us, length us, event | category | flops | bytes accessed | tf_op | source)
XLA Modules:
  0.0 25.5 jit_solution(5218516533120138114)
XLA Ops:
  0.0 24.8 %step.1 = f32[5,125,128]{2,1,0:T(8,128)S(1)} custom-call(f32[5,125,128]{2,1,0:T(8,128)} %refs_0_.1, f32[3,128]{1,0:T(4,128)} %refs_1_.1, s32[3,128]{1,0:T(4,128)} %refs_2_.1, s32[3,128]{1,0:T(4,128)} %refs_3_.1, s32[1,1024]{1,0:T(1,128)} %refs_4_.1, f32[3,5,1,1024]{3,2,1,0:T(1,128)} %bitcast.1, s32[1,600]{1,0:T(1,128)} %refs_6_.1, ...), custom_call_target="tpu_custom_call" | custom-call | tf_op jit(solution)/shard_map/step/pallas_call | solution.py:545
  24.8 0.7 %copy.12 = f32[5,125,128]{2,1,0:T(8,128)} copy(f32[5,125,128]{2,1,0:T(8,128)S(1)} %step.1) | data formatting | bytes 640000

commit v8 on v7

--- a/solution.py
+++ b/solution.py
@@ -462,7 +462,7 @@
     loads[4].wait()
     loads[5].wait()
 
-    late = (near == tiles // 2) | (near == tiles // 2 + 1)
+    late = (near >= tiles // 2) & (near <= tiles // 2 + 2)
 
     @pl.when(late)
     def _():

time: 25.7 us -> 25.6 us (level)
  no operation moved by 1% of the time
where the time goes in v8:
time: 25.6 us; the launch traced here: 25.4 us
  Pallas kernels  24.7 us (96%)
  local copies, waits for them, and re-layouts  0.73 us (3%)
    pallas_call x1, Pallas kernels, body(): pl.pallas_call(functools.partial(kernel, grids, parts), out_shape=jax.Sha...  24.7 us
    unnamed x1, local copies, waits for them, and re-layouts  0.73 us

profile of v8, /device:TPU:1, one launch (start us, length us, event | category | flops | bytes accessed | tf_op | source)
XLA Modules:
  0.0 25.4 jit_solution(15802538916191891498)
XLA Ops:
  0.0 24.7 %step.1 = f32[5,125,128]{2,1,0:T(8,128)S(1)} custom-call(f32[5,125,128]{2,1,0:T(8,128)} %refs_0_.1, f32[3,128]{1,0:T(4,128)} %refs_1_.1, s32[3,128]{1,0:T(4,128)} %refs_2_.1, s32[3,128]{1,0:T(4,128)} %refs_3_.1, s32[1,1024]{1,0:T(1,128)} %refs_4_.1, f32[3,5,1,1024]{3,2,1,0:T(1,128)} %bitcast.1, s32[1,600]{1,0:T(1,128)} %refs_6_.1, ...), custom_call_target="tpu_custom_call" | custom-call | tf_op jit(solution)/shard_map/step/pallas_call | solution.py:545
  24.7 0.7 %copy.12 = f32[5,125,128]{2,1,0:T(8,128)} copy(f32[5,125,128]{2,1,0:T(8,128)S(1)} %step.1) | data formatting | bytes 640000
